TPU v7x, 32 devices: a whole 2x2x4 slice. The times are simulated.
32 devices in a mesh: dp: 16 (over z, y, core), tensor: 2 (over x).
Axes of the slice: x: 2, y: 2, z: 4, core: 2. Of those that a mesh axis runs over, the one named last changes fastest.
Arguments:
- patches: bfloat16 [37632, 768], P(('dp', 'tensor')), may hold values from -6 to 6
- gain_first: bfloat16 [768], replicated, may hold values from 0.099609375 to 1.8984375
- shift_first: bfloat16 [768], replicated, may hold values from -3 to 3
- attend_weight: bfloat16 [768, 2304], P(None, 'tensor'), may hold values from -0.21875 to 0.21875
- attend_bias: bfloat16 [24, 2, 32], P('tensor'), may hold values from -3 to 3
- offset_table: bfloat16 [24, 169], P('tensor'), may hold values from -5 to 5
- output_weight: bfloat16 [768, 768], P('tensor'), may hold values from -0.625 to 0.625
- output_bias: bfloat16 [768], replicated, may hold values from -3 to 3
- gain_second: bfloat16 [768], replicated, may hold values from 0.099609375 to 1.8984375
- shift_second: bfloat16 [768], replicated, may hold values from -3 to 3
- expand_weight: bfloat16 [768, 3072], P(None, 'tensor'), may hold values from -0.21875 to 0.21875
- expand_bias: bfloat16 [3072], P('tensor'), may hold values from -3 to 3
- reduce_weight: bfloat16 [3072, 768], P('tensor'), may hold values from -0.109375 to 0.109375
- reduce_bias: bfloat16 [768], replicated, may hold values from -3 to 3
- crop_counts: int32 [96], P('dp'), may hold values from 2 to 10, as said below
- cotangent: bfloat16 [37632, 768], P(('dp', 'tensor')), may hold values from -6 to 6
Outputs:
- result: bfloat16 [37632, 768], P(('dp', 'tensor'))
- input_grad: float32 [37632, 768], P(('dp', 'tensor'))
- gain_first_grad: float32 [768], P('tensor')
- shift_first_grad: float32 [768], P('tensor')
- attend_weight_grad: float32 [768, 2304], P(None, 'tensor')
- attend_bias_grad: float32 [24, 2, 32], P('tensor')
- offset_table_grad: float32 [24, 169], P('tensor')
- output_weight_grad: float32 [768, 768], P('tensor')
- output_bias_grad: float32 [768], P('tensor')
- gain_second_grad: float32 [768], P('tensor')
- shift_second_grad: float32 [768], P('tensor')
- expand_weight_grad: float32 [768, 3072], P(None, 'tensor')
- expand_bias_grad: float32 [3072], P('tensor')
- reduce_weight_grad: float32 [3072, 768], P('tensor')
- reduce_bias_grad: float32 [768], P('tensor')
Inputs may be any that keep to these rules, and one draw needn't show every extreme that they name: `crop_counts`: in each index of dp the counts of its 6 images sum to exactly 36, so their 2 + count windows fill its 48 window slots in order.
All inputs are finite; a program needn't handle non-finite values.
Results may differ from a plain program's by a relative error of at most 0.02.
Values may be sent and summed in bfloat16 or wider, within the bound.
No kernel may reach another device: no remote copies, remote signals or barrier semaphores. Data moves between devices by JAX's collectives and lax.ppermute only.
A program may use at most 256 MiB of HBM per device.

v0:
```python
from functools import partial

import jax
import jax.numpy as jnp
import numpy as np
from jax import lax
from jax.experimental import pallas as pl
from jax.experimental.pallas import tpu as pltpu
from jax.sharding import Mesh
from jax.sharding import PartitionSpec as P

HEAD_DIM = 32
EPSILON = 1e-05
MASKED = 30000.0
SIDE = 7
SLOTS = SIDE * SIDE
BLK = 128
GROUP = 4
GW = 3 * GROUP * HEAD_DIM
BF = jnp.bfloat16
F32 = jnp.float32
VMEM_LIMIT = 60 * 1024 * 1024


def dot(a, b):
    return jnp.dot(a, b, preferred_element_type=F32)


def dot_nt(a, b):
    return lax.dot_general(a, b, (((1,), (1,)), ((), ())), preferred_element_type=F32)


def dot_tn(a, b):
    return lax.dot_general(a, b, (((0,), (0,)), ((), ())), preferred_element_type=F32)


def kind_tables():
    slot = -np.ones((2, BLK), np.int64)
    owner = 100 + np.arange(BLK)[None].repeat(2, 0)
    nine = np.arange(9)
    nine = (nine // 3) * SIDE + nine % 3
    for w in range(2):
        slot[0, w * SLOTS : (w + 1) * SLOTS] = np.arange(SLOTS)
        owner[0, w * SLOTS : (w + 1) * SLOTS] = w
    for w in range(3):
        at = 2 * SLOTS + 9 * w
        slot[0, at : at + 9] = nine
        owner[0, at : at + 9] = 2 + w
    for w in range(14):
        slot[1, 9 * w : 9 * w + 9] = nine
        owner[1, 9 * w : 9 * w + 9] = w
    pick = (slot[:, :, None] == np.arange(64)[None, None, :]).astype(np.float32)
    same = owner[:, :, None] == owner[:, None, :]
    mask = np.where(same, 0.0, -1e30).astype(np.float32)
    return pick, mask


def stride_tables():
    slot, _ = kind_tables()
    s = np.where(slot.sum(2) > 0, slot.argmax(2), -1)
    place = np.where(s >= 0, 13 * (s // SIDE) + s % SIDE, -1)
    up = (place[:, :, None] == np.arange(BLK)).astype(np.float32)
    down = ((84 - place)[:, :, None] == np.arange(BLK)) & (place >= 0)[:, :, None]
    return up, down.astype(np.float32).transpose(0, 2, 1)


def group_perm():
    perm = np.zeros((GW, GW), np.float32)
    for h in range(GROUP):
        for p in range(3):
            for e in range(HEAD_DIM):
                perm[(h * 3 + p) * HEAD_DIM + e, (p * GROUP + h) * HEAD_DIM + e] = 1.0
    return perm


PLAN_HEAD = 8
G1, B1, G2, B2, OB, RB = (slice(i, i + 1) for i in range(6))
AT_C, AT_ME = 6, 7


def bound_kernel(w, bias, table, out):
    width = w.shape[1]
    q = jnp.zeros((1, BLK), F32)
    k = jnp.zeros((1, BLK), F32)
    for start in range(0, width, BLK):
        size = min(BLK, width - start)
        x = w[:, start : start + size]
        gram = dot_tn(x, x)
        a = lax.broadcasted_iota(jnp.int32, (size, size), 0) >> 5
        b = lax.broadcasted_iota(jnp.int32, (size, size), 1) >> 5
        sums = jnp.sum(jnp.where(a == b, gram * gram, 0.0), axis=0, keepdims=True)
        lane = lax.broadcasted_iota(jnp.int32, (1, size), 1) >> 5
        for i in range(size // HEAD_DIM):
            part = (start // HEAD_DIM + i) % 3
            top = jnp.max(jnp.where(lane == i, sums, 0.0), axis=1, keepdims=True)
            if part == 0:
                q = jnp.maximum(q, top)
            if part == 1:
                k = jnp.maximum(k, top)
    qb = bias[...].astype(F32)
    col = lax.broadcasted_iota(jnp.int32, qb.shape, 1)
    qb = jnp.sum(jnp.where(col < HEAD_DIM, qb * qb, 0.0), axis=1, keepdims=True)
    qb = jnp.max(qb, axis=0, keepdims=True)
    top = jnp.max(jnp.max(jnp.abs(table[...].astype(F32)), axis=1, keepdims=True), axis=0, keepdims=True)
    out[...] = jnp.zeros_like(out)
    for i, v in enumerate((q, k, qb, top)):
        out[i : i + 1, :] = jnp.broadcast_to(v, (1, BLK))


def plan_kernel(windows, images, per_chunk, where, counts, bounds, vecs, out):
    d = vecs.shape[1]
    g1, b1 = vecs.at[G1], vecs.at[B1]
    big = bounds[...]

    def root4(v):
        return jnp.sqrt(jnp.sqrt(HEAD_DIM * v))

    reach = jnp.sqrt(float(d)) * jnp.max(jnp.abs(g1[...]), axis=1, keepdims=True)
    reach = 1.02 * (reach + jnp.sqrt(jnp.sum(b1[...] * b1[...], axis=1, keepdims=True)))
    q = 1.01 * (reach * root4(big[0:1, :]) + jnp.sqrt(big[2:3, :])) * HEAD_DIM**-0.5
    top = 1.01 * q * (reach * root4(big[1:2, :])) + big[3:4, :]
    safe = jnp.where(2.0 * top < MASKED - 500.0, 1, 0)
    bad = 1 - jnp.min(safe)
    first = where[0]
    nf = jnp.int32(0)
    nq = jnp.int32(0)
    for i in range(2 * windows + PLAN_HEAD, out.shape[0]):
        out[i] = 0
    for w in range(windows):
        place = first + w
        start = jnp.int32(0)
        offset = jnp.int32(-1)
        for i in range(images):
            total = counts[i] + 2
            inside = (place >= start) & (place < start + total)
            offset = jnp.where(inside, place - start, offset)
            start = start + total
        present = offset >= 0
        whole = present & (offset < 2)
        full = present & (whole | (bad > 0))
        part = present & (~whole) & (bad == 0)
        out[PLAN_HEAD + 2 * windows + w] = whole.astype(jnp.int32)

        @pl.when(full)
        def _():
            out[PLAN_HEAD + nf] = w

        @pl.when(part)
        def _():
            out[PLAN_HEAD + windows + nq] = w

        nf = nf + full.astype(jnp.int32)
        nq = nq + part.astype(jnp.int32)
    n0 = (nf + 1) >> 1
    left = jnp.maximum(nq - 3 * n0, 0)
    n1 = jnp.int32(0)
    for i in range(-(-windows // 14)):
        n1 = n1 + (left > 14 * i).astype(jnp.int32)
    nb = n0 + n1
    chunks = jnp.int32(1)
    for i in range(1, windows):
        chunks = chunks + (nb > per_chunk * i).astype(jnp.int32)
    for i, v in enumerate((nb, n0, chunks, bad, nf, nq, where[1], where[2])):
        out[i] = v


def norm_stats(x):
    mean = jnp.mean(x, axis=1, keepdims=True)
    c = x - mean
    scale = lax.rsqrt(jnp.mean(c * c, axis=1, keepdims=True) + EPSILON)
    return c * scale, scale


def norm_back(grad, normal, scale, gain):
    inner = grad * gain
    mean = jnp.mean(inner, axis=1, keepdims=True)
    proj = jnp.mean(inner * normal, axis=1, keepdims=True)
    return scale * (inner - mean - normal * proj)


def gather_kernel(windows, meta, slots, patches, cot, vecs, xc, cotc, branch, first, live, idx_row, idx, pick):
    rows = xc.shape[0]
    total = patches.shape[0]
    blocks = rows // BLK
    spots = lax.broadcasted_iota(jnp.int32, (BLK, total), 1)
    chunk = pl.program_id(0)
    n0 = meta[1]
    r = lax.broadcasted_iota(jnp.int32, (BLK, 1), 0)

    def listed(first_at, count, i):
        ok = (i >= 0) & (i < count)
        w = meta[first_at + jnp.where(ok, i, 0)]
        return jnp.where(ok, w, -1)

    def spread(ends, wins):
        base = jnp.full((BLK, 1), -1, jnp.int32)
        for end, w in reversed(list(zip(ends, wins))):
            base = jnp.where(r < end, w, base)
        return base

    def one(b, carry):
        at = pl.ds(pl.multiple_of(b * BLK, BLK), BLK)
        block = chunk * blocks + b
        kind0 = block < n0

        @pl.when(kind0)
        def _():
            wins = [listed(PLAN_HEAD, meta[4], 2 * block + i) for i in range(2)]
            wins += [listed(PLAN_HEAD + windows, meta[5], 3 * block + i) for i in range(3)]
            ends = [SLOTS, 2 * SLOTS] + [2 * SLOTS + 9 * (i + 1) for i in range(3)]
            base = spread(ends, wins)
            slot = slots[0]
            where_whole = [
                jnp.where(w >= 0, meta[PLAN_HEAD + 2 * windows + jnp.maximum(w, 0)], 0) for w in wins[:2]
            ] + [jnp.int32(1)] * 3
            sure = spread(ends, where_whole) > 0
            ok = base >= 0
            idx[...] = jnp.where(ok, base * SLOTS + slot, -1)
            live[at, :] = jnp.where(ok & (sure | (slots[2] > 0)), 1.0, 0.0)

        @pl.when(jnp.logical_not(kind0))
        def _():
            start = 3 * n0 + 14 * (block - n0)
            wins = [listed(PLAN_HEAD + windows, meta[5], start + i) for i in range(14)]
            base = spread([9 * (i + 1) for i in range(14)], wins)
            ok = base >= 0
            idx[...] = jnp.where(ok, base * SLOTS + slots[1], -1)
            live[at, :] = jnp.where(ok, 1.0, 0.0)

        here = idx[...]
        wide = jnp.broadcast_to(here.astype(F32), (BLK, BLK))
        idx_row[0, :, at] = wide.T[0:1, :].astype(jnp.int32)
        pick[at, :] = (spots == here).astype(F32).astype(BF)
        return carry

    lax.fori_loop(0, blocks, one, 0)
    x = dot(pick[...], patches[...])
    xc[...] = x.astype(BF)
    up = dot(pick[...], cot[...])
    cotc[...] = up.astype(BF)
    branch[...] = (up * live[...]).astype(BF)
    for b in range(blocks):
        at = slice(b * BLK, (b + 1) * BLK)
        n, _ = norm_stats(xc[at, :].astype(F32))
        first[at, :] = (n * vecs[G1] + vecs[B1]).astype(BF)


def lane_head(shape, axis):
    return lax.broadcasted_iota(jnp.int32, shape, axis) >> 5


def spread_rows(x):
    h = lane_head(x.shape, 1)
    zero = jnp.zeros_like(x)
    return jnp.concatenate([jnp.where(h == i, x, zero) for i in range(GROUP)], axis=0)


def spread_cols(xt):
    h = lane_head(xt.shape, 0)
    zero = jnp.zeros_like(xt)
    return jnp.concatenate([jnp.where(h == i, xt, zero) for i in range(GROUP)], axis=1)


def fold_rows(x):
    h = lane_head((BLK, BLK), 1)
    out = x[0:BLK]
    for i in range(1, GROUP):
        out = jnp.where(h == i, x[i * BLK : (i + 1) * BLK], out)
    return out


def attend_kernel(pieces, groups, tail, prior, meta, live, first, perm, pick, mask, bias, rel, *rest):
    w, rest = rest[:pieces], rest[pieces:]
    if tail:
        (xc, vecs), rest = rest[:2], rest[2:]
        before, rest = rest[:prior], rest[prior:]
        w_before, rest = rest[:prior], rest[prior:]
        w_out, rest = rest[:pieces], rest[pieces:]
        qkv, probs, mixed_out, middle, second, table, mixed, att = rest
    else:
        qkv, probs, mixed_out, table = rest
    rows, d = first.shape
    blocks = rows // BLK
    chunk, step = pl.program_id(0), pl.program_id(1)
    c = meta[AT_C]
    n0 = meta[1]
    near = pl.ds(pl.multiple_of(c * (d // 2), BLK), d // 2)
    far = pl.ds(pl.multiple_of((1 - c) * (d // 2), BLK), d // 2)

    @pl.when(step < groups)
    def _():
        if pieces == 1:
            v = dot(first[...], w[0][...])
        else:
            v = dot(first[:, near], w[0][...]) + dot(first[:, far], w[1][...])
        v = v + bias[...]
        block = lax.broadcasted_iota(jnp.int32, (1, GW), 1) >> 5
        is_q = block == 0
        for i in range(3, 3 * GROUP, 3):
            is_q = is_q | (block == i)
        v = (v * jnp.where(is_q, HEAD_DIM**-0.5, 1.0)).astype(BF)
        qkv[...] = dot(v, perm[...]).astype(BF)
        places = []
        for h in range(GROUP):
            row = rel[pl.ds(step * GROUP + h, 1), :]
            row = pltpu.roll(jnp.broadcast_to(row, (BLK, 2 * BLK)), 2 * BLK - 88, 1, stride=1, stride_axis=0)
            places.append(row[:, 0:BLK].astype(BF))
        for kind in range(2):
            e = pick[kind]
            for h in range(GROUP):
                half = dot(e, places[h]).astype(BF)
                t = dot_nt(half, e) + mask[kind].astype(F32)
                table[kind, h * BLK : (h + 1) * BLK, :] = t.astype(BF)
        for b in range(blocks):
            at = slice(b * BLK, (b + 1) * BLK)
            kind = jnp.where(chunk * blocks + b < n0, 0, 1)
            q = qkv[at, 0:BLK]
            k = qkv[at, BLK : 2 * BLK]
            v = qkv[at, 2 * BLK : 3 * BLK]
            st = dot_nt(spread_rows(k), q) + table[kind].astype(F32)
            dead = (live[at, :] - 1.0) * MASKED
            st = st.reshape(GROUP, BLK, BLK) + jnp.where(meta[3] > 0, dead, 0.0)[None]
            peak = jnp.max(st, axis=1, keepdims=True)
            e = jnp.exp(st - peak)
            p = (e * (1.0 / jnp.sum(e, axis=1, keepdims=True))).astype(BF)
            p = p.reshape(GROUP * BLK, BLK)
            probs[b, 0] = p
            vt = v.astype(F32).T.astype(BF)
            m = dot(spread_cols(vt), p).T.astype(BF)
            mixed_out[at, :] = m
            if tail:
                mixed[at, pl.ds(pl.multiple_of(step * BLK, BLK), BLK)] = m

    if not tail:
        return

    @pl.when(step == groups)
    def _():
        if pieces == 1:
            att[...] = dot(mixed[...], w_out[0][...])
        else:
            att[:, near] = dot(mixed[...], w_out[0][...])
            att[:, far] = dot(mixed[...], w_out[1][...])
        for m, v in zip(before, w_before):
            att[...] = att[...] + dot(m[...], v[...])
        for b in range(blocks):
            at = slice(b * BLK, (b + 1) * BLK)
            m = xc[at, :].astype(F32) + live[at, :] * (att[at, :] + vecs[OB])
            middle[at, :] = m
            nrm, _ = norm_stats(m)
            second[at, :] = (nrm * vecs[G2] + vecs[B2]).astype(BF)


def feed_kernel(tiles, pieces, last, prior, meta, second, branch, *rest):
    we, wr, rest = rest[:pieces], rest[pieces : 2 * pieces], rest[2 * pieces :]
    be, rest = rest[0], rest[1:]
    if last:
        (live, middle, cotc, vecs), rest = rest[:4], rest[4:]
        sg_in, rest = rest[:prior], rest[prior:]
    grads, rest = rest[:tiles], rest[tiles:]
    dbe, red = rest[:2]
    if last:
        (mg, ag, vec), rest = rest[2:5], rest[5:]
    else:
        (sg,), rest = rest[2:3], rest[3:]
    sec, br, e_buf, r_buf, gbuf, ra, sa, half, sem, w_sem, g_sem = rest[:11]
    if last:
        mid_buf, cot_buf, live_buf, sg_buf = rest[11:]
    ch, d = sec.shape
    wide = e_buf.shape[2]
    c0, me = meta[AT_C], meta[AT_ME]
    y = me & 1
    chunks = meta[2]

    def move(a, b, i):
        return pltpu.make_async_copy(a, b, sem.at[i])

    def loads(c):
        rows = pl.ds(pl.multiple_of(c * ch, ch), ch)
        return [move(second.at[rows, :], sec, 0), move(branch.at[rows, :], br, 1)]

    def weights(i):
        if pieces == 1:
            at = pl.ds(pl.multiple_of((i ^ c0) * wide, BLK), wide)
            a, b = we[0].at[:, at], wr[0].at[at, :]
        else:
            a, b = we[i], wr[i]
        return [
            pltpu.make_async_copy(a, e_buf.at[i], w_sem.at[2 * i]),
            pltpu.make_async_copy(b, r_buf.at[i], w_sem.at[2 * i + 1]),
        ]

    def extras(c):
        rows = pl.ds(pl.multiple_of(c * ch, ch), ch)
        out = [
            move(middle.at[rows, :], mid_buf, 2),
            move(cotc.at[rows, :], cot_buf, 3),
            move(live.at[rows, :], live_buf, 4),
        ]
        return out + [move(x.at[rows, :], sg_buf, 5) for x in sg_in]

    def store(i):
        return pltpu.make_async_copy(gbuf.at[i], grads[i], g_sem.at[i])

    if last:
        vec[...] = jnp.zeros_like(vec)

    def chunk(c, carry):
        rows = pl.ds(pl.multiple_of(c * ch, ch), ch)
        for x in loads(c):
            x.start()

        @pl.when(c == 0)
        def _():
            for i in range(tiles):
                for x in weights(i):
                    x.start()

        if last:
            for x in extras(c):
                x.start()
        for x in loads(c):
            x.wait()

        def tile(t, carry):
            for i in range(tiles):

                @pl.when((t == i) & (c == 0))
                def _():
                    for x in weights(i):
                        x.wait()

            at = pl.ds(pl.multiple_of((t ^ c0) * wide, BLK), wide)
            e, r = e_buf[t], r_buf[t]
            u = dot(sec[...], e) + be[:, at]
            cdf = 0.5 * (1.0 + lax.erf(u * 0.7071067811865476))
            h = (u * cdf).astype(BF)
            slope = cdf + u * (jnp.exp(-0.5 * u * u) * 0.3989422804014327)
            pg = (dot_nt(br[...], r) * slope).astype(BF)
            grad_b = jnp.sum(pg.astype(F32), axis=0, keepdims=True)

            def put(low, g):
                n = wide // 2
                for i in range(2):
                    ref = gbuf.at[t, i ^ y, low : low + d, :]
                    part = g[:, i * n : (i + 1) * n]

                    @pl.when(c == 0)
                    def _():
                        ref[...] = part.astype(BF)

                    @pl.when(c > 0)
                    def _():
                        ref[...] = (ref[...].astype(F32) + part).astype(BF)

            put(0, dot_tn(sec[...], pg))
            put(d, dot_tn(br[...], h))

            @pl.when(c == 0)
            def _():
                dbe[:, at] = grad_b

            @pl.when(c > 0)
            def _():
                dbe[:, at] = dbe[:, at] + grad_b

            red_t = dot(h, r)
            sg_t = dot_nt(pg, e)

            @pl.when(t == 0)
            def _():
                ra[...] = red_t
                sa[...] = sg_t

            @pl.when(t > 0)
            def _():
                ra[...] = ra[...] + red_t
                sa[...] = sa[...] + sg_t

            for i in range(tiles):

                @pl.when((t == i) & (c == chunks - 1))
                def _():
                    store(i).start()

            return carry

        lax.fori_loop(0, tiles, tile, 0)
        half[0] = ra[...].astype(BF)
        outs = [move(half.at[0], red.at[rows, :], 0)]
        outs[0].start()
        if not last:
            half[1] = sa[...].astype(BF)
            outs.append(move(half.at[1], sg.at[rows, :], 1))
            outs[1].start()
        else:
            for x in extras(c):
                x.wait()
            for b in range(ch // BLK):
                at = slice(b * BLK, (b + 1) * BLK)
                nrm, scale = norm_stats(mid_buf[at, :])
                g = sa[at, :]
                if prior:
                    g = g + sg_buf[at, :].astype(F32)
                m = cot_buf[at, :].astype(F32) + norm_back(g, nrm, scale, vecs[G2])
                ra[at, :] = m
                kept = m * live_buf[at, :]
                half[1, at, :] = kept.astype(BF)
                vec[0:1, :] = vec[0:1, :] + jnp.sum(g * nrm, axis=0, keepdims=True)
                vec[1:2, :] = vec[1:2, :] + jnp.sum(g, axis=0, keepdims=True)
                vec[2:3, :] = vec[2:3, :] + jnp.sum(kept, axis=0, keepdims=True)
            outs += [move(half.at[1], ag.at[rows, :], 1), move(ra, mg.at[rows, :], 2)]
            for x in outs[1:]:
                x.start()
        for x in outs:
            x.wait()
        return carry

    lax.fori_loop(0, chunks, chunk, 0)
    for i in range(tiles):
        store(i).wait()


def back_kernel(pieces, groups, split, meta, ag, perm, pick, pick_t, qkv, probs, mixed, first, *rest):
    w_out, rest = rest[:pieces], rest[pieces:]
    dqkv, rest = rest[0], rest[1:]
    grads, rest = rest[: 2 if split else 1], rest[2 if split else 1 :]
    dba, drel, dperm, dmix, table = rest
    rows, d = ag.shape
    blocks = rows // BLK
    step, chunk = pl.program_id(0), pl.program_id(1)
    n0 = meta[1]
    c, me = meta[AT_C], meta[AT_ME]
    half = d // 2
    stays = (step >> 1) == (me >> 1)

    def put(ref, value):
        @pl.when(chunk == 0)
        def _():
            ref[...] = value.astype(ref.dtype)

        @pl.when(chunk > 0)
        def _():
            ref[...] = (ref[...].astype(F32) + value).astype(ref.dtype)

    def put_grad(low, high, value):
        if not split:
            put(grads[0].at[0, low:high, :], value)
            return

        @pl.when(stays)
        def _():
            put(grads[0].at[0, low:high, :], value)

        @pl.when(jnp.logical_not(stays))
        def _():
            put(grads[1].at[0, low:high, :], value)

    @pl.when(step == groups)
    def _():
        wide = groups * BLK
        for i in range(2):
            put_grad(i * wide, (i + 1) * wide, dot_tn(mixed[...], ag[:, i * half : (i + 1) * half]))

    @pl.when(step < groups)
    def _():
        @pl.when(chunk == 0)
        def _():
            table[...] = jnp.zeros_like(table)

        if pieces == 1:
            dmix[...] = dot_nt(ag[...], w_out[0][...]).astype(BF)
        else:
            near = pl.ds(pl.multiple_of(c * half, BLK), half)
            far = pl.ds(pl.multiple_of((1 - c) * half, BLK), half)
            dmix[...] = (dot_nt(ag[:, near], w_out[0][...]) + dot_nt(ag[:, far], w_out[1][...])).astype(BF)
        for b in range(blocks):
            at = slice(b * BLK, (b + 1) * BLK)
            kind = jnp.where(chunk * blocks + b < n0, 0, 1)
            q = qkv[at, 0:BLK]
            k = qkv[at, BLK : 2 * BLK]
            v = qkv[at, 2 * BLK : 3 * BLK]
            do = dmix[at, :]
            p = probs[b, 0]
            dp = dot_nt(spread_rows(v), do).reshape(GROUP, BLK, BLK)
            pf = p.astype(F32).reshape(GROUP, BLK, BLK)
            x = pf * dp
            ds = x - pf * jnp.sum(x, axis=1, keepdims=True)
            ds = ds.astype(BF).reshape(GROUP * BLK, BLK)
            table[kind] = table[kind] + ds.astype(F32)
            dv = fold_rows(dot(p, do))
            dk = fold_rows(dot(ds, q))
            kt = k.astype(F32).T.astype(BF)
            dq = (dot(spread_cols(kt), ds) * HEAD_DIM**-0.5).T
            dperm[at, 0:BLK] = dq.astype(BF)
            dperm[at, BLK : 2 * BLK] = dk.astype(BF)
            dperm[at, 2 * BLK : 3 * BLK] = dv.astype(BF)
        x = dot_nt(dperm[...], perm[...]).astype(BF)
        dqkv[...] = x
        put_grad(0, d, dot_tn(first[...], x))
        put(dba, jnp.sum(x.astype(F32), axis=0, keepdims=True))

        @pl.when(chunk == meta[2] - 1)
        def _():
            for h in range(GROUP):
                total = jnp.zeros((BLK, BLK), F32)
                for kind in range(2):
                    a = table[kind, h * BLK : (h + 1) * BLK, :]
                    a = dot(a.astype(BF), pick[kind]).astype(BF)
                    total = total + dot(pick_t[kind], a)
                wide = jnp.concatenate([total, jnp.zeros_like(total)], axis=1)
                wide = pltpu.roll(wide, 0, 1, stride=1, stride_axis=0)
                drel[pl.ds(step * GROUP + h, 1), :] = jnp.sum(wide, axis=0, keepdims=True)


def row_tiles(rows, size=384):
    return [(a, min(size, rows - a)) for a in range(0, rows, size)]


def ends_kernel(pieces, meta, live, xc, cotc, middle, mg, vecs, *rest):
    n = len(pieces)
    red, rest = rest[:n], rest[n:]
    dqkv, rest = rest[:n], rest[n:]
    w = []
    for k in pieces:
        w.append(rest[:k])
        rest = rest[k:]
    res, hi, lo, vec, fg = rest
    rows, d = xc.shape
    blocks = rows // BLK
    chunk = pl.program_id(0)
    c = meta[AT_C]
    half = d // 2

    @pl.when(chunk == 0)
    def _():
        vec[...] = jnp.zeros_like(vec)

    for s in range(n):
        if len(w[s]) == 1:
            v = dot_nt(dqkv[s][...], w[s][0][...])
            fg[...] = v if s == 0 else fg[...] + v
        else:
            for i in range(2):
                cols = pl.ds(pl.multiple_of((c if i == 0 else 1 - c) * half, BLK), half)
                fg[:, cols] = fg[:, cols] + dot_nt(dqkv[s][...], w[s][i][...])

    for b in range(blocks):
        at = slice(b * BLK, (b + 1) * BLK)
        keep = live[at, :]
        nrm, scale = norm_stats(xc[at, :].astype(F32))
        g = fg[at, :]
        up = cotc[at, :].astype(F32)
        delta = mg[at, :] - up + norm_back(g, nrm, scale, vecs[G1])
        top = delta.astype(BF)
        hi[at, :] = top
        lo[at, :] = (delta - top.astype(F32)).astype(BF)
        reduced = vecs[RB]
        for x in red:
            reduced = reduced + x[at, :].astype(F32)
        res[at, :] = (middle[at, :] + keep * reduced).astype(BF)
        vec[0:1, :] = vec[0:1, :] + jnp.sum(g * nrm, axis=0, keepdims=True)
        vec[1:2, :] = vec[1:2, :] + jnp.sum(g, axis=0, keepdims=True)
        vec[2:3, :] = vec[2:3, :] + jnp.sum(up * keep, axis=0, keepdims=True)


def scatter_kernel(meta, idx, res, hi, lo, patches, cot, result, input_grad):
    rows = res.shape[0]
    chunk = pl.program_id(0)
    for start, size in row_tiles(patches.shape[0]):
        at = slice(start, start + size)
        spots = start + lax.broadcasted_iota(jnp.int32, (size, rows), 0)
        hit = (spots == idx[0]).astype(F32)
        here = jnp.sum(hit, axis=1, keepdims=True) > 0.0
        put = hit.astype(BF)
        new = dot(put, res[...])
        grad = dot(put, hi[...]) + dot(put, lo[...])

        @pl.when(chunk == 0)
        def _():
            result[at, :] = jnp.where(here, new, patches[at, :].astype(F32)).astype(BF)
            input_grad[at, :] = cot[at, :].astype(F32) + grad

        @pl.when(chunk > 0)
        def _():
            result[at, :] = jnp.where(here, new, result[at, :].astype(F32)).astype(BF)
            input_grad[at, :] = input_grad[at, :] + grad


SMEM = pl.BlockSpec(memory_space=pltpu.SMEM)
ANY = pl.BlockSpec(memory_space=pl.ANY)
PACK = 24


def pack_kernel(where, v1, v2, *refs):
    n = 2
    db, dba, drel = (refs[i * n : (i + 1) * n] for i in range(3))
    outs = refs[3 * n :]
    d = v1.shape[1]
    half = d // 2
    for s in range(n):
        t = where[0] if s == 0 else 1 - where[0]
        cols = pl.ds(pl.multiple_of(t * half, BLK), half)
        out = outs[s]
        out[...] = jnp.zeros_like(out)
        out[0:1, :] = db[s][...].astype(BF).astype(F32)
        out[1:2, 0 : dba[s].shape[1]] = dba[s][...]
        for i, (v, r) in enumerate(((v1, 0), (v1, 1), (v2, 2), (v2, 0), (v2, 1), (v1, 2))):
            out[2 + i : 3 + i, 0:half] = v[r : r + 1, cols]
        k = drel[s].shape[0]
        out[8 : 8 + k, 0 : drel[s].shape[1]] = drel[s][...]


def pack(t, v1, v2, db, dba, drel):
    v = pl.BlockSpec(memory_space=pltpu.VMEM)
    shape = sds((PACK, db[0].shape[1]), F32)
    return pl.pallas_call(
        pack_kernel,
        in_specs=[SMEM] + [v] * 8,
        out_specs=[v, v],
        out_shape=[shape, shape],
        name="pack",
    )(t, v1, v2, *db, *dba, *drel)


def relative_z(z, ids):
    r = z ^ ids[2]
    return 2 * (r & 1) + (r >> 1)


def place_feed_kernel(ids, a, b, c, e, exp, red):
    @pl.when(pl.program_id(0) < 4)
    def _():
        exp[...] = a[0, 0].astype(F32)
        red[...] = b[0, 0].astype(F32).T

    @pl.when(pl.program_id(0) >= 4)
    def _():
        exp[...] = c[0, 0].astype(F32)
        red[...] = e[0, 0].astype(F32).T


def place_feed(ids, near, far, d, hidden):
    def spec(which, odd):
        def at(j, ids):
            j = jnp.minimum(j, 3) if which == 0 else jnp.maximum(j, 4)
            return ((j >> 1) & 1) ^ ids[1], relative_z(2 * (j & 1) + odd, ids), 0, 0

        return pl.BlockSpec((1, 1, GW, GW), at)

    tile = lambda j, ids: ((j >> 2) ^ ids[0]) * 2 + ((j >> 1) & 1)
    return pl.pallas_call(
        place_feed_kernel,
        grid_spec=pltpu.PrefetchScalarGridSpec(
            num_scalar_prefetch=1,
            grid=(8,),
            in_specs=[spec(0, 0), spec(0, 1), spec(1, 0), spec(1, 1)],
            out_specs=[
                pl.BlockSpec((GW, GW), lambda j, ids: (j & 1, tile(j, ids))),
                pl.BlockSpec((GW, GW), lambda j, ids: (tile(j, ids), j & 1)),
            ],
        ),
        out_shape=[sds((d, hidden), F32), sds((hidden, d), F32)],
        name="place_feed",
    )(ids, near, near, far, far)


def place_attend_kernel(ids, *refs):
    att, out = refs[8:]
    for i in range(4):
        near, far = refs[i], refs[4 + i]
        x = jnp.where((i >> 1) == ids[0], near[0, 0], far[0, 0]).astype(F32)
        if i < 3:
            att[:, i * GW : (i + 1) * GW] = x
        else:
            out[...] = x


def place_attend(ids, near, far, d):
    r = near.shape[2]
    ins = [
        pl.BlockSpec(
            (1, 1, r, GW),
            lambda q, ids, i=i: (relative_z((q & 1) * 2 + (q >> 1), ids), (i & 1) ^ ids[1], 0, 0),
        )
        for i in range(4)
    ]
    return pl.pallas_call(
        place_attend_kernel,
        grid_spec=pltpu.PrefetchScalarGridSpec(
            num_scalar_prefetch=1,
            grid=(4,),
            in_specs=ins + ins,
            out_specs=[
                pl.BlockSpec((r, 3 * GW), lambda q, ids: (q, 0)),
                pl.BlockSpec((r, GW), lambda q, ids: (q & 1, q >> 1)),
            ],
        ),
        out_shape=[sds((d, 3 * GW), F32), sds((GW, d), F32)],
        name="place_attend",
    )(ids, near, near, near, near, far, far, far, far)


def guarded(body, axis):
    def run(meta, *refs):
        @pl.when(pl.program_id(axis) < meta[2])
        def _():
            body(meta, *refs)

    return run


def clamp(i, meta):
    return jnp.minimum(i, meta[2] - 1)


def whole_spec(shape):
    zeros = (0,) * len(shape)
    return pl.BlockSpec(shape, lambda *_: zeros, pipeline_mode=pl.Buffered(1))


def chunk_spec(shape):
    zeros = (0,) * (len(shape) - 1)
    return pl.BlockSpec(shape, lambda i, meta: (clamp(i, meta),) + zeros)


def sds(shape, dtype):
    return jax.ShapeDtypeStruct(shape, dtype)


def w_(a):
    return (a, whole_spec(a.shape))


def o_(shape, dtype):
    return (sds(shape, dtype), whole_spec(shape))


class Local:
    def __init__(self, rows):
        self.rows = rows
        self.windows = rows // SLOTS
        worst = (self.windows + 1) // 2
        self.per_chunk = min(5, max(worst, 1))
        self.chunks = -(-worst // self.per_chunk)
        self.ch = self.per_chunk * BLK
        self.all = self.ch * self.chunks
        pick, mask = kind_tables()
        self.mask = jnp.asarray(mask, BF)
        self.perm = jnp.asarray(group_perm(), BF)
        up, down_t = stride_tables()
        self.up, self.down_t = jnp.asarray(up, BF), jnp.asarray(down_t, BF)
        slot = np.where(pick.sum(2) > 0, pick.argmax(2), 0)
        corner = (slot[0] // SIDE < 3) & (slot[0] % SIDE < 3)
        self.slots = jnp.asarray(np.stack([slot[0], slot[1], corner])[:, :, None], jnp.int32)

    def row(self, k, dt):
        return (sds((self.all, k), dt), chunk_spec((self.ch, k)))

    def c(self, a):
        return (a, chunk_spec((self.ch,) + a.shape[1:]))

    def call(self, body, name, ins, outs, scratch=(), grid=None, axis=0, flops=0, size=0, limit=VMEM_LIMIT):
        f = pl.pallas_call(
            body if axis is None else guarded(body, axis),
            out_shape=[o for o, _ in outs],
            grid_spec=pltpu.PrefetchScalarGridSpec(
                num_scalar_prefetch=1,
                grid=(self.chunks,) if grid is None else grid,
                in_specs=[s for _, s in ins],
                out_specs=[s for _, s in outs],
                scratch_shapes=list(scratch),
            ),
            compiler_params=pltpu.CompilerParams(vmem_limit_bytes=limit),
            cost_estimate=pl.CostEstimate(flops=int(flops), bytes_accessed=int(size), transcendentals=0),
            name=name,
        )
        return f(self.meta, *[a for a, _ in ins])

    def bound(self, w, bias, table):
        ins = [w, bias.reshape(bias.shape[0], -1), table]
        return pl.pallas_call(
            bound_kernel,
            out_shape=sds((8, BLK), F32),
            compiler_params=pltpu.CompilerParams(vmem_limit_bytes=VMEM_LIMIT),
            name="bound",
        )(*ins)

    def plan(self, place, counts, bounds, vecs):
        v = pl.BlockSpec(memory_space=pltpu.VMEM)
        self.meta = pl.pallas_call(
            partial(plan_kernel, self.windows, counts.shape[0], self.per_chunk),
            out_shape=sds((PLAN_HEAD + 3 * self.windows,), jnp.int32),
            in_specs=[SMEM, SMEM, v, v],
            out_specs=SMEM,
            name="plan",
        )(place, counts, bounds, vecs)

    def gather(self, patches, cot, vecs):
        ch, d = self.ch, patches.shape[1]
        idx = (sds((self.chunks, 1, ch), jnp.int32), pl.BlockSpec((1, 1, ch), lambda i, meta: (clamp(i, meta), 0, 0)))
        return self.call(
            partial(gather_kernel, self.windows),
            "gather_rows",
            [w_(self.slots), w_(patches), w_(cot), w_(vecs)],
            [self.row(d, BF)] * 4 + [self.row(1, F32), idx],
            [pltpu.VMEM((BLK, 1), jnp.int32), pltpu.VMEM((ch, self.rows), BF)],
            flops=4 * ch * self.rows * d,
            size=8 * self.rows * d,
        )

    def attend(self, live, first, bias, rel, w, tail=None, before=()):
        ch, d = self.ch, first.shape[1]
        width = w[0].shape[1]
        groups = width // GW
        clip = lambda i, g, meta: jnp.where(i < meta[2], jnp.minimum(g, groups - 1), groups - 1)
        by_chunk = lambda a: (a, pl.BlockSpec((ch,) + a.shape[1:], lambda i, g, meta: (clamp(i, meta), 0)))
        cols = lambda a, k: (a, pl.BlockSpec((a.shape[0], k), lambda i, g, meta: (0, clip(i, g, meta))))
        out = lambda total, k, dt: (
            sds((self.all, total), dt),
            pl.BlockSpec((ch, k), lambda i, g, meta: (clamp(i, meta), clip(i, g, meta))),
        )
        pshape = (self.per_chunk * self.chunks, groups, GROUP * BLK, BLK)
        pspec = pl.BlockSpec((self.per_chunk, 1) + pshape[2:], lambda i, g, meta: (clamp(i, meta), clip(i, g, meta), 0, 0))
        ins = [by_chunk(live), by_chunk(first), w_(self.perm), w_(self.up), w_(self.mask), cols(bias, GW), w_(rel)]
        ins += [cols(a, GW) for a in w]
        outs = [out(width, GW, BF), (sds(pshape, BF), pspec), out(groups * BLK, BLK, BF)]
        scratch = [pltpu.VMEM((2, GROUP * BLK, BLK), BF)]
        steps = groups
        if tail is not None:
            steps += 1
            xc, vecs, wo = tail
            ins += [by_chunk(xc), w_(vecs)]
            ins += [by_chunk(m) for m, _ in before] + [w_(a) for _, a in before] + [w_(a) for a in wo]
            outs += [
                (sds((self.all, d), dt), pl.BlockSpec((ch, d), lambda i, g, meta: (clamp(i, meta), 0)))
                for dt in (F32, BF)
            ]
            scratch += [pltpu.VMEM((ch, groups * BLK), BF), pltpu.VMEM((ch, d), F32)]
        return self.call(
            partial(attend_kernel, len(w), groups, tail is not None, len(before)),
            "attend",
            ins,
            outs,
            scratch,
            grid=(self.chunks, steps),
            flops=0.16 * ch * d * width,
            size=0.4 * ch * d,
        )

    def feed(self, second, branch, we, wr, be, last=None):
        ch, d = self.ch, second.shape[1]
        hidden = be.shape[1]
        pieces = len(we)
        wide = 2 * GW
        tiles = hidden // wide
        any_ = lambda a: (a, ANY)
        full = lambda dt: (sds((self.all, d), dt), ANY)
        ins = [any_(a) for a in (second, branch, *we, *wr)] + [w_(be)]
        outs = [(sds((2, 2 * d, GW), BF), ANY)] * tiles + [o_((1, hidden), F32), full(BF)]
        v = pltpu.VMEM
        scratch = [v((ch, d), BF)] * 2 + [v((tiles, d, wide), BF), v((tiles, wide, d), BF)]
        scratch += [v((tiles, 2, 2 * d, GW), BF), v((ch, d), F32), v((ch, d), F32), v((2, ch, d), BF)]
        dma = pltpu.SemaphoreType.DMA
        scratch += [dma((6,)), dma((2 * tiles,)), dma((tiles,))]
        prior = 0
        if last is None:
            outs += [full(BF)]
        else:
            live, middle, cotc, vecs, sums = last
            prior = len(sums)
            ins += [any_(live), any_(middle), any_(cotc), w_(vecs)] + [any_(a) for a in sums]
            outs += [full(F32), full(BF), o_((8, d), F32)]
            scratch += [v((ch, d), F32), v((ch, d), BF), v((ch, 1), F32), v((ch, d), BF)]
        return self.call(
            partial(feed_kernel, tiles, pieces, last is not None, prior),
            "feed",
            ins,
            outs,
            scratch,
            grid=(1,),
            axis=None,
            flops=12 * ch * d * hidden,
            size=8 * d * hidden,
        )

    def back(self, ag, qkv, probs, mixed, first, wo):
        ch, d = self.ch, first.shape[1]
        width = qkv.shape[1]
        groups = width // GW
        split = groups == 3
        clip = lambda g: jnp.minimum(g, groups - 1)
        by_chunk = lambda a: (a, pl.BlockSpec((ch,) + a.shape[1:], lambda g, i, meta: (clamp(i, meta), 0)))
        cols = pl.BlockSpec((ch, GW), lambda g, i, meta: (clamp(i, meta), clip(g)))
        pspec = pl.BlockSpec((self.per_chunk, 1) + probs.shape[2:], lambda g, i, meta: (clamp(i, meta), clip(g), 0, 0))
        one = (1, 2 * groups * BLK, GW)
        if split:

            def tile(start):
                return lambda g, i, meta: (
                    (jnp.clip(g - start(meta[AT_ME] >> 1), 0, 1) ^ meta[AT_ME]) & 1,
                    0,
                    0,
                )

            shape = sds((2,) + one[1:], BF)
            grads = [(shape, pl.BlockSpec(one, tile(lambda h: 2 * h))), (shape, pl.BlockSpec(one, tile(lambda h: 2 - 2 * h)))]
        else:
            grads = [(sds((groups + 1,) + one[1:], BF), pl.BlockSpec(one, lambda g, i, meta: (g, 0, 0)))]
        rows = lambda a, k: pl.BlockSpec((k, a), lambda g, i, meta: (clip(g), 0))
        return self.call(
            partial(back_kernel, len(wo), groups, split),
            "back",
            [by_chunk(ag), w_(self.perm), w_(self.up), w_(self.down_t), (qkv, cols), (probs, pspec)]
            + [by_chunk(mixed), by_chunk(first)]
            + [(a, rows(a.shape[1], BLK)) for a in wo],
            [(sds((self.all, width), BF), cols), *grads]
            + [(sds((1, width), F32), pl.BlockSpec((1, GW), lambda g, i, meta: (0, clip(g))))]
            + [o_((groups * GROUP, 2 * BLK), F32)],
            [pltpu.VMEM((ch, GW), BF), pltpu.VMEM((ch, BLK), BF), pltpu.VMEM((2, GROUP * BLK, BLK), F32)],
            grid=(groups + 1, self.chunks),
            axis=1,
            flops=14 * ch * d * width,
            size=30 * ch * d,
        )

    def ends(self, live, xc, cotc, middle, mg, vecs, red, dqkv, ws):
        ch, d = self.ch, xc.shape[1]
        c = self.c
        return self.call(
            partial(ends_kernel, [len(a) for a in ws]),
            "ends",
            [c(live), c(xc), c(cotc), c(middle), c(mg), w_(vecs)]
            + [c(a) for a in (*red, *dqkv)]
            + [w_(a) for s in ws for a in s],
            [self.row(d, BF)] * 3 + [o_((8, d), F32)],
            [pltpu.VMEM((ch, d), F32)],
            flops=6 * ch * d * d,
            size=30 * ch * d,
        )

    def scatter(self, idx, res, hi, lo, patches, cot):
        ch, d = self.ch, patches.shape[1]
        rspec = (idx, pl.BlockSpec((1, 1, ch), lambda i, meta: (clamp(i, meta), 0, 0)))
        return self.call(
            scatter_kernel,
            "scatter",
            [rspec, self.c(res), self.c(hi), self.c(lo), w_(patches), w_(cot)],
            [o_(patches.shape, BF), o_(patches.shape, F32)],
            flops=6 * ch * self.rows * d,
            size=12 * self.rows * d,
        )


CODES = 169


def pad_table(table):
    return jnp.pad(table.astype(F32), ((0, 0), (4, 2 * BLK - CODES - 4)))


def bias_row(bias):
    b = bias.astype(F32)
    return jnp.stack([b[:, 0], jnp.zeros_like(b[:, 0]), b[:, 1]], axis=1).reshape(1, -1)


def pick_half(a, bit, axis=0):
    n = a.shape[axis] // 2
    return lax.dynamic_slice_in_dim(a, bit * n, n, axis)


def swap(a, axis, n, step=1):
    return lax.ppermute(a, axis, [(i, i ^ step) for i in range(n)])


def plus(*xs):
    total = xs[0].astype(F32)
    for x in xs[1:]:
        total = total + x.astype(F32)
    return total.astype(BF)


def after(x, *deps):
    return lax.optimization_barrier((x, *deps))[0]


def on_device(
    nz,
    nt,
    patches,
    gain_first,
    shift_first,
    attend_weight,
    attend_bias,
    offset_table,
    output_weight,
    output_bias,
    gain_second,
    shift_second,
    expand_weight,
    expand_bias,
    reduce_weight,
    reduce_bias,
    crop_counts,
    cotangent,
):
    fast = nt == 2 and nz == 4
    t, c, y, z = (lax.axis_index(a) for a in ("tensor", "core", "y", "z"))
    rows, d = patches.shape
    local = Local(rows)
    vec = lambda a: a.astype(F32).reshape(1, -1)
    vecs = jnp.stack([gain_first, shift_first, gain_second, shift_second, output_bias, reduce_bias]).astype(F32)
    bound = local.bound(attend_weight, attend_bias, offset_table)
    if fast:
        got, w_att_in, w_out_in = lax.optimization_barrier(
            (swap(bound, "tensor", nt), attend_weight, output_weight)
        )
        bound = jnp.maximum(bound, got)
        x_att = swap(pick_half(pick_half(w_att_in, c), y), "tensor", nt)
        x_out = swap(pick_half(w_out_in, c, 1), "tensor", nt)
        small = lambda a: [a, swap(a, "tensor", nt)]
        me = c * 2 + y
    else:
        w_att = [[lax.all_gather(attend_weight, "tensor", axis=1, tiled=True)]]
        w_out = [[lax.all_gather(output_weight, "tensor", axis=0, tiled=True)]]
        w_exp = [[lax.all_gather(expand_weight, "tensor", axis=1, tiled=True)]]
        w_red = [[lax.all_gather(reduce_weight, "tensor", axis=0, tiled=True)]]
        bound = lax.pmax(bound, "tensor")
        small = lambda a: [lax.all_gather(a, "tensor", axis=0, tiled=True)]
        me = c = 0 * c
    place = jnp.stack([t * local.windows, c, me]).astype(jnp.int32)
    local.plan(place, crop_counts, bound, vecs)
    bias, rel, b_exp = small(attend_bias), small(pad_table(offset_table)), small(expand_bias)
    xc, cotc, branch, first, live, idx = local.gather(patches, cotangent, vecs)

    if fast:
        xc, first, x_att, x_out, bias, rel, b_exp = lax.optimization_barrier(
            (xc, first, x_att, x_out, bias, rel, b_exp)
        )
    bias, b_exp = [bias_row(b) for b in bias], [vec(a) for a in b_exp]
    if fast:
        s_exp = after(pick_half(pick_half(expand_weight, c, 1), y, 1), x_att)
        first, s_exp = lax.optimization_barrier((first, s_exp))
        x_exp = swap(s_exp, "tensor", nt)
        y_att = swap(x_att, "y", 2)
        w_out = [[output_weight], [x_out, swap(x_out, "core", 2)]]
        qkv0, probs0, mixed0 = local.attend(live, first, bias[0], rel[0], [attend_weight])
        y_att, x_exp, mixed0 = lax.optimization_barrier((y_att, x_exp, mixed0))
        x_att = jnp.where(y == 0, jnp.concatenate([x_att, y_att], 0), jnp.concatenate([y_att, x_att], 0))
        w_att = [[attend_weight], [x_att, swap(x_att, "core", 2)]]
        y_exp = swap(x_exp, "y", 2)
        first, s_red = lax.optimization_barrier((first, after(pick_half(reduce_weight, c, 0), w_att[1][0])))
        x_red = swap(s_red, "tensor", nt)
        held = [(qkv0, probs0, mixed0)]
        before = [(mixed0, output_weight)]
    else:
        held, before = [], []
    qkv1, probs1, mixed1, middle, second = local.attend(
        live, first, bias[-1], rel[-1], w_att[-1], (xc, vecs, w_out[-1]), before
    )
    held.append((qkv1, probs1, mixed1))
    n = len(w_att)

    def bias_grad(a):
        a = a.reshape(-1, 3, HEAD_DIM)
        return jnp.stack([a[:, 0], a[:, 2]], axis=1)

    if fast:
        y_exp, x_red, second = lax.optimization_barrier((y_exp, x_red, second))
        x_exp = jnp.where(y == 0, jnp.concatenate([x_exp, y_exp], 1), jnp.concatenate([y_exp, x_exp], 1))
        second, x_exp = lax.optimization_barrier((second, x_exp))
        k0, s0, db0, red0, sg0 = local.feed(second, branch, [expand_weight], [reduce_weight], b_exp[0])
        e1 = [x_exp, swap(x_exp, "core", 2)]
        r1 = [x_red, swap(x_red, "core", 2)]
        k1, s1, db1, red1, mg, ag, v2 = local.feed(second, branch, e1, r1, b_exp[1], (live, middle, cotc, vecs, [sg0]))
        def split(keep, got):
            h = keep.shape[1] // 2
            return [plus(keep[:, i * h : (i + 1) * h], got[:, i * h : (i + 1) * h]) for i in range(2)]

        def first_leg(own, peer):
            return swap(peer[0], "tensor", nt), swap(jnp.stack([own[1][1], peer[1][1]]), "y", 2)

        def second_leg(own, peer, gx, gy):
            low = plus(own[0][1], gx[1])
            up = plus(own[0][0], gx[0])
            peer_b = plus(peer[1][0], gy[1])
            own_b = plus(own[1][0], gy[0])
            return up, swap(low, "y", 2), own_b, swap(peer_b, "tensor", nt)

        def z_first(up, gy, own_b, gx):
            a, b = plus(up, gy), plus(own_b, gx)
            return jnp.where(z % 2 == 0, a, b), jnp.where(z % 2 == 0, b, a)

        def z_second(keep, got):
            hi = z // 2
            total = lambda i: plus(pick_half(keep, i), pick_half(got, i))
            return total(hi), total(1 - hi)

        ff_peer = split(k1, swap(s1, "core", 2))
        ff_own = split(k0, swap(s0, "core", 2))
        ag, *ff = lax.optimization_barrier((ag, *ff_own, *ff_peer))
        ff_own, ff_peer = ff[:2], ff[2:]
        fx, fy = first_leg(ff_own, ff_peer)
        dq1, gk1, gs1, dba1, drel1 = local.back(ag, *held[1], first, w_out[1])
        fx, fy, dq1, gs1, ag = lax.optimization_barrier((fx, fy, dq1, gs1, ag))
        ff_up, fy, ff_b, fx = second_leg(ff_own, ff_peer, fx, fy)
        got1 = swap(gs1, "core", 2)
        dq0, gk0, gs0, dba0, drel0 = local.back(ag, *held[0], first, w_out[0])
        got1, fx, fy, dq0, gs0 = lax.optimization_barrier((got1, fx, fy, dq0, gs0))
        at_peer = split(gk1, got1)
        at_own = split(gk0, swap(gs0, "core", 2))
        ax, ay = first_leg(at_own, at_peer)
        ff_keep, ff_send = z_first(ff_up, fy, ff_b, fx)
        ff_got = swap(ff_send, "z", nz, 1)
        mg, *at4, ff_keep, ff_send = lax.optimization_barrier((mg, *at_own, *at_peer, ff_keep, ff_send))
        res, hi, lo, v1 = local.ends(live, xc, cotc, middle, mg, vecs, [red0, red1], [dq0, dq1], w_att)
        ax, ay, ff_got, res = lax.optimization_barrier((ax, ay, ff_got, res))
        up, ay, own_b, ax = second_leg(at_own, at_peer, ax, ay)
        ff_keep, ff_send = z_second(ff_keep, ff_got)
        ff_got = swap(ff_send, "z", nz, 2)
        v1, up, own_b, ff_keep, ff_send = lax.optimization_barrier((v1, up, own_b, ff_keep, ff_send))
        mine, other = pack(t.reshape(1).astype(jnp.int32), v1, v2, (db0, db1), (dba0, dba1), (drel0, drel1))
        ff_got, ax, ay, mine, other = lax.optimization_barrier((ff_got, ax, ay, mine, other))
        ids = jnp.stack([c, y, z]).astype(jnp.int32)
        keep, send = z_first(up, ay, own_b, ax)
        got = swap(send, "z", nz, 1)
        ff = plus(ff_keep, ff_got)
        ff2 = swap(ff, "z", nz, 2)
        tiny = plus(mine, swap(other.astype(BF), "tensor", nt))
        keep, ff, got, tiny = lax.optimization_barrier((keep, ff, got, tiny))
        keep, send = z_second(keep, got)
        got = swap(send, "z", nz, 2)
        tiny = plus(tiny, swap(tiny, "core", 2))
        keep, send, ff2, got, tiny = lax.optimization_barrier((keep, send, ff2, got, tiny))
        ff = jnp.stack([ff, ff2])
        att = plus(keep, got)
        ff1 = swap(ff, "z", nz, 1)
        att_y = swap(att, "y", 2)
        tiny = plus(tiny, swap(tiny, "y", 2))
        ff, att, att_y, tiny = lax.optimization_barrier((ff, att, att_y, tiny))
        att = jnp.stack([att, att_y])
        att2 = swap(att, "z", nz, 2)
        tiny = plus(tiny, swap(tiny, "z", nz, 1))
        att, ff1, tiny = lax.optimization_barrier((att, ff1, tiny))
        ff = jnp.concatenate([ff, ff1], 0)
        ffy = swap(ff, "y", 2)
        tiny = plus(tiny, swap(tiny, "z", nz, 2))
        ff, att2, tiny, res = lax.optimization_barrier((ff, att2, tiny, res))
        att = jnp.stack([att, att2])
        att1 = swap(att, "z", nz, 1)
        att, res = lax.optimization_barrier((att, res))
        result, input_grad = local.scatter(idx, res, hi, lo, patches, cotangent)
        att1, ffy, result = lax.optimization_barrier((att1, ffy, result))
        att = jnp.concatenate([att, att1], 0)
        att_far = swap(att, "core", 2)
        ff, ffy, att_far = lax.optimization_barrier((ff, ffy, att_far))
        ff = jnp.stack([ff, ffy])
        far = swap(ff, "core", 2)
        g_att, g_out = place_attend(ids, att, att_far, d)
        g_exp, g_red = place_feed(ids, ff, far, d, 4 * GW)
        tiny = tiny.astype(F32)
        gb_exp, gb_att = tiny[0], bias_grad(tiny[1, : 3 * GW])
        vectors, g_rel = tiny[2:8, : d // 2], tiny[8 : 8 + drel0.shape[0], :CODES]
    else:
        *tiles, gb_exp, red, mg, ag, v2 = local.feed(second, branch, w_exp[0], w_red[0], b_exp[0], (live, middle, cotc, vecs, []))
        dq, ga, dba, drel = local.back(ag, *held[0], first, w_out[0])
        res, hi, lo, v1 = local.ends(live, xc, cotc, middle, mg, vecs, [red], [dq], w_att)
        result, input_grad = local.scatter(idx, res, hi, lo, patches, cotangent)
        ff = jnp.concatenate(tiles, 0)
        g_exp = ff[:, 0:d].transpose(1, 0, 2).reshape(d, -1)
        g_red = ff[:, d:].transpose(0, 2, 1).reshape(-1, d)
        g_att = ga[0 : dq.shape[1] // GW, 0:d].transpose(1, 0, 2).reshape(d, -1)
        g_out = ga[dq.shape[1] // GW].reshape(2, d, d // 2).transpose(1, 0, 2).reshape(d, d)
        dp = ("z", "y", "core")

        def total(a, axis):
            a = lax.psum_scatter(a.astype(BF), "tensor", scatter_dimension=axis, tiled=True)
            return lax.psum(a, dp).astype(F32)

        vectors = total(jnp.stack([v1[0], v1[1], v2[2], v2[0], v2[1], v1[2]]), 1)
        gb_att, g_rel, gb_exp = total(bias_grad(dba), 0), total(drel[:, :CODES], 0), total(gb_exp[0], 0)
        g_exp, g_att, g_out, g_red = total(g_exp, 1), total(g_att, 1), total(g_out, 0), total(g_red, 0)

    return (
        result,
        input_grad,
        vectors[0],
        vectors[1],
        g_att,
        gb_att,
        g_rel,
        g_out,
        vectors[2],
        vectors[3],
        vectors[4],
        g_exp,
        gb_exp,
        g_red,
        vectors[5],
    )


def solution(mesh):
    nt = mesh.shape["tensor"]
    nz = mesh.shape["dp"] // 4
    grid = Mesh(mesh.devices.reshape(nz, 2, 2, nt), ("z", "y", "core", "tensor"))
    dp = ("z", "y", "core")
    rows = P(dp + ("tensor",), None)
    in_specs = (
        rows,
        P(),
        P(),
        P(None, "tensor"),
        P("tensor", None, None),
        P("tensor", None),
        P("tensor", None),
        P(),
        P(),
        P(),
        P(None, "tensor"),
        P("tensor"),
        P("tensor", None),
        P(),
        P(dp),
        rows,
    )
    out_specs = (
        rows,
        rows,
        P("tensor"),
        P("tensor"),
        P(None, "tensor"),
        P("tensor", None, None),
        P("tensor", None),
        P("tensor", None),
        P("tensor"),
        P("tensor"),
        P("tensor"),
        P(None, "tensor"),
        P("tensor"),
        P("tensor", None),
        P("tensor"),
    )
    return jax.shard_map(partial(on_device, nz, nt), mesh=grid, in_specs=in_specs, out_specs=out_specs, check_vma=False)
```

profile of v0, /device:TPU:0, one launch (start us, length us, event | category | flops | bytes accessed | tf_op | source)
XLA Modules:
  0.0 332.2 jit_solution(9007587638417183633)
XLA Ops:
  0.7 3.0 collective-permute-start.3
  5.1 2.9 bound.1
  19.5 9.2 %gather_rows.1 = (bf16[1920,768]{1,0:T(8,128)(2,1)}, bf16[1920,768]{1,0:T(8,128)(2,1)}, bf16[1920,768]{1,0:T(8,128)(2,1)}, bf16[1920,768]{1,0:T(8,128)(2,1)}, f32[1920,1]{1,0:T(8,128)}, /*index=5*/s32[3,1,640]{2,1,0:T(1,128)}) custom-call(s32[80]{0:T(128)} %plan.1.meta, s32[3,128,1]{2,1,0:T(8,128)} %constant.95.clone.refs_0_, bf16[1176,768]{1,0:T(8,128)(2,1)} %refs_4_.3, ...), custom_call_target="tpu_custom_call" | custom-call | flops 2312110080 | bytes 7225344 | tf_op jit(solution)/shard_map/gather_rows/pallas_call | solution.py:878
  28.8 3.0 collective-permute-done.2.refs_13_.refs_8_
  37.8 11.6 %attend.2 = (bf16[1920,1152]{1,0:T(8,128)(2,1)}, bf16[15,3,512,128]{3,2,1,0:T(8,128)(2,1)}, bf16[1920,384]{1,0:T(8,128)(2,1)}) custom-call(s32[80]{0:T(128)} %plan.1.meta, f32[1920,1]{1,0:T(8,128)} %get-tuple-element.148.refs_0_.rest_5_, bf16[1920,768]{1,0:T(8,128)(2,1)} %get-tuple-element.165.refs_1_.refs_7_, ...), custom_call_target="tpu_custom_call" | custom-call | flops 90596968 | bytes 196608 | tf_op jit(solution)/shard_map/attend/pallas_call | solution.py:878
  54.4 17.9 %attend.3 = (bf16[1920,1152]{1,0:T(8,128)(2,1)}, bf16[15,3,512,128]{3,2,1,0:T(8,128)(2,1)}, bf16[1920,384]{1,0:T(8,128)(2,1)}, f32[1920,768]{1,0:T(8,128)}, bf16[1920,768]{1,0:T(8,128)(2,1)}) custom-call(s32[80]{0:T(128)} %plan.1.meta, f32[1920,1]{1,0:T(8,128)} %get-tuple-element.148.refs_0_.rest_5_, bf16[1920,768]{1,0:T(8,128)(2,1)} %get-tuple-element.165.refs_1_.refs_7_, ...), custom_call_target="tpu_custom_call" | custom-call | flops 90596968 | bytes 196608 | tf_op jit(solution)/shard_map/attend/pallas_call | solution.py:878
  72.3 2.6 collective-permute-done.11.rest_2_
  78.2 20.3 %feed.2 = (bf16[2,1536,384]{2,1,0:T(8,128)(2,1)}, bf16[2,1536,384]{2,1,0:T(8,128)(2,1)}, f32[1,1536]{1,0:T(1,128)}, bf16[1920,768]{1,0:T(8,128)(2,1)}, bf16[1920,768]{1,0:T(8,128)(2,1)}) custom-call(s32[80]{0:T(128)} %plan.1.meta, bf16[1920,768]{1,0:T(8,128)(2,1)} %get-tuple-element.176.second, bf16[1920,768]{1,0:T(8,128)(2,1)} %get-tuple-element.177.branch, ...), custom_call_target="tpu_custom_call" | custom-call | flops 9059696640 | bytes 9437184 | tf_op jit(solution)/shard_map/feed/pallas_call | solution.py:878
  98.7 21.8 %feed.3 = (bf16[2,1536,384]{2,1,0:T(8,128)(2,1)}, bf16[2,1536,384]{2,1,0:T(8,128)(2,1)}, f32[1,1536]{1,0:T(1,128)}, bf16[1920,768]{1,0:T(8,128)(2,1)}, f32[1920,...) custom-call(s32[80]{0:T(128)} %plan.1.meta, bf16[1920,768]{1,0:T(8,128)(2,1)} %get-tuple-element.176.second, ...), custom_call_target="tpu_custom_call" | custom-call | flops 9059696640 | bytes 9437184 | tf_op jit(solution)/shard_map/feed/pallas_call | solution.py:878
  122.5 3.1 add_convert_fusion.2
  129.7 20.4 %back.2 = (bf16[1920,1152]{1,0:T(8,128)(2,1)}, bf16[2,768,384]{2,1,0:T(8,128)(2,1)}, bf16[2,768,384]{2,1,0:T(8,128)(2,1)}, f32[1,1152]{1,0:T(1,128)}, f32[12,256]{1,0:T(8,128)}) custom-call(s32[80]{0:T(128)} %plan.1.meta, bf16[1920,768]{1,0:T(8,128)(2,1)} %get-tuple-element.198.refs_0_, bf16[384,384]{1,0:T(8,128)(2,1)} %constant.92.clone.refs_2_.refs_1_, ...), custom_call_target="tpu_custom_call" | custom-call | flops 7927234560 | bytes 14745600 | tf_op jit(solution)/shard_map/back/pallas_call | solution.py:878
  150.2 6.8 %collective-permute-done.17 = bf16[2,768,384]{2,1,0:T(8,128)(2,1)} collective-permute-done((bf16[2,768,384]{2,1,0:T(8,128)(2,1)}, bf16[2,768,384]{2,1,0:T(8,128)(2,1)}, u32[]{:S(2)}, u32[]{:S(2)}) %collective-permute-start.17) | collective-permute-done | bytes 1179680 | tf_op jit(solution)/shard_map/ppermute | solution.py:1073
  163.3 20.9 %back.3 = (bf16[1920,1152]{1,0:T(8,128)(2,1)}, bf16[2,768,384]{2,1,0:T(8,128)(2,1)}, bf16[2,768,384]{2,1,0:T(8,128)(2,1)}, f32[1,1152]{1,0:T(1,128)}, f32[12,256]{1,0:T(8,128)}) custom-call(s32[80]{0:T(128)} %plan.1.meta, bf16[1920,768]{1,0:T(8,128)(2,1)} %get-tuple-element.198.refs_0_, bf16[384,384]{1,0:T(8,128)(2,1)} %constant.92.clone.refs_2_.refs_1_, ...), custom_call_target="tpu_custom_call" | custom-call | flops 7927234560 | bytes 14745600 | tf_op jit(solution)/shard_map/back/pallas_call | solution.py:878
  184.4 2.8 add_convert_fusion.6
  188.8 2.9 broadcast_select_fusion.1
  196.4 13.3 %ends.1 = (bf16[1920,768]{1,0:T(8,128)(2,1)}, bf16[1920,768]{1,0:T(8,128)(2,1)}, bf16[1920,768]{1,0:T(8,128)(2,1)}, f32[8,768]{1,0:T(8,128)}) custom-call(s32[80]{0:T(128)} %plan.1.meta, f32[1920,1]{1,0:T(8,128)} %get-tuple-element.148.refs_0_.rest_5_, bf16[1920,768]{1,0:T(8,128)(2,1)} %get-tuple-element.153.refs_9_.refs_1_, ...), custom_call_target="tpu_custom_call" | custom-call | flops 2264924160 | bytes 14745600 | tf_op jit(solution)/shard_map/ends/pallas_call | solution.py:878
  215.4 2.6 collective-permute-start.25
  219.6 2.4 collective-permute-done.27
  223.0 7.4 %collective-permute-done.25 = bf16[384,384]{1,0:T(8,128)(2,1)S(1)} collective-permute-done((bf16[384,384]{1,0:T(8,128)(2,1)S(1)}, bf16[384,384]{1,0:T(8,128)(2,1)S(1)}, u32[]{:S(2)}, u32[]{:S(2)}) %collective-permute-start.25) | collective-permute-done | bytes 294944 | tf_op jit(solution)/shard_map/ppermute | solution.py:1073
  233.2 3.2 collective-permute-start.30
  236.5 10.4 %collective-permute-done.28 = bf16[384,384]{1,0:T(8,128)(2,1)S(1)} collective-permute-done((bf16[384,384]{1,0:T(8,128)(2,1)S(1)}, bf16[384,384]{1,0:T(8,128)(2,1)S(1)}, u32[]{:S(2)}, u32[]{:S(2)}) %collective-permute-start.28) | collective-permute-done | bytes 294944 | tf_op jit(solution)/shard_map/ppermute | solution.py:1073
  249.2 7.8 %collective-permute-done.31 = bf16[192,384]{1,0:T(8,128)(2,1)S(1)} collective-permute-done((bf16[192,384]{1,0:T(8,128)(2,1)S(1)}, bf16[192,384]{1,0:T(8,128)(2,1)S(1)}, u32[]{:S(2)}, u32[]{:S(2)}) %collective-permute-start.31) | collective-permute-done | bytes 147488 | tf_op jit(solution)/shard_map/ppermute | solution.py:1073
  259.3 2.8 collective-permute-done.34
  262.2 2.3 collective-permute-done.33
  264.5 11.1 %collective-permute-done.36 = bf16[24,1536]{1,0:T(8,128)(2,1)S(1)} collective-permute-done((bf16[24,1536]{1,0:T(8,128)(2,1)S(1)}, bf16[24,1536]{1,0:T(8,128)(2,1)S(1)}, u32[]{:S(2)}, u32[]{:S(2)}) %collective-permute-start.36) | collective-permute-done | bytes 73760 | tf_op jit(solution)/shard_map/ppermute | solution.py:1073
  277.0 2.5 collective-permute-start.37
  279.5 9.1 %collective-permute-done.38 = bf16[24,1536]{1,0:T(8,128)(2,1)S(1)} collective-permute-done((bf16[24,1536]{1,0:T(8,128)(2,1)S(1)}, bf16[24,1536]{1,0:T(8,128)(2,1)S(1)}, u32[]{:S(2)}, u32[]{:S(2)}) %collective-permute-start.38) | collective-permute-done | bytes 73760 | tf_op jit(solution)/shard_map/ppermute | solution.py:1073
  289.2 4.4 %collective-permute-done.37 = bf16[2,192,384]{2,1,0:T(8,128)(2,1)S(1)} collective-permute-done((bf16[2,192,384]{2,1,0:T(8,128)(2,1)S(1)}, bf16[2,192,384]{2,1,0:T(8,128)(2,1)S(1)}, u32[]{:S(2)}, u32[]{:S(2)}) %collective-permute-start.37) | collective-permute-done | bytes 294944 | tf_op jit(solution)/shard_map/ppermute | solution.py:1073
  293.8 13.6 %scatter.1 = (bf16[1176,768]{1,0:T(8,128)(2,1)}, f32[1176,768]{1,0:T(8,128)}) custom-call(s32[80]{0:T(128)} %plan.1.meta, s32[3,1,640]{2,1,0:T(1,128)} %get-tuple-element.259.refs_0_, bf16[1920,768]{1,0:T(8,128)(2,1)} %get-tuple-element.261.refs_1_, bf16[1920,768]{1,0:T(8,128)(2,1)} %get-tuple-element.262.refs_2_, ...), custom_call_target="tpu_custom_call" | custom-call | flops 3468165120 | bytes 10838016 | tf_op jit(solution)/shard_map/scatter/pallas_call | solution.py:878
  308.0 2.8 collective-permute-done.41.refs_4_.refs_5_.refs_6_.refs_7_
  317.1 6.1 %place_attend.1 = (f32[768,1152]{1,0:T(8,128)}, f32[384,768]{1,0:T(8,128)}) custom-call(s32[3]{0:T(128)} %pad_add_fusion.1.ids, bf16[4,2,192,384]{3,2,1,0:T(8,128)(2,1)} %copy-done, bf16[4,2,192,384]{3,2,1,0:T(8,128)(2,1)} %copy-done, bf16[4,2,192,384]{3,2,1,0:T(8,128)(2,1)} %copy-done, bf16[4,2,192,384]{3,2,1,0:T(8,128)(2,1)} %copy-done, ...), custom_call_target="tpu_custom_call" | custom-call | tf_op jit(solution)/shard_map/place_attend/pallas_call | solution.py:788
  323.2 8.8 %place_feed.1 = (f32[768,1536]{1,0:T(8,128)}, f32[1536,768]{1,0:T(8,128)}) custom-call(s32[3]{0:T(128)} %pad_add_fusion.1.ids, bf16[2,4,384,384]{3,2,1,0:T(8,128)(2,1)} %copy-done.1, bf16[2,4,384,384]{3,2,1,0:T(8,128)(2,1)} %copy-done.1, bf16[2,4,384,384]{3,2,1,0:T(8,128)(2,1)} %collective-permute-done.42.c.e, ...), custom_call_target="tpu_custom_call" | custom-call | tf_op jit(solution)/shard_map/place_feed/pallas_call | solution.py:752
  (206 shorter events, 70.7 us)
Async XLA Ops:
  0.7 28.0 %collective-permute-start.3 = (bf16[12,2,32]{2,1,0:T(2,128)(2,1)}, bf16[12,2,32]{2,1,0:T(2,128)(2,1)S(1)}, u32[]{:S(2)}, u32[]{:S(2)}) collective-permute-start(bf16[12,2,32]{2,1,0:T(2,128)(2,1)} %param.25), channel_id=1, source_target_pairs={{0,1},{1,0},{2,3},{3,2},{4,5},{5,4},{6,7},{7,6},{8,9},{9,8},{10,11... | collective-permute-start | bytes 4616 | tf_op jit(solution)/shard_map/ppermute | solution.py:1073
  8.0 20.7 %collective-permute-start.5 = (bf16[1536]{0:T(1024)(128)(2,1)S(1)}, bf16[1536]{0:T(1024)(128)(2,1)S(1)}, u32[]{:S(2)}, u32[]{:S(2)}) collective-permute-start(bf16[1536]{0:T(1024)(128)(2,1)S(1)} %copy-done.24), channel_id=1, source_target_pairs={{0,1},{1,0},{2,3},{3,2},{4,5},{5,4},{6,7},{7,6},{8,9},{9,8},{10,11... | collective-permute-start | bytes 9224 | tf_op jit(solution)/shard_map/ppermute | solution.py:1073
  10.1 18.6 %collective-permute-start.4 = (f32[12,256]{1,0:T(8,128)S(1)}, f32[12,256]{1,0:T(8,128)S(1)}, u32[]{:S(2)}, u32[]{:S(2)}) collective-permute-start(f32[12,256]{1,0:T(8,128)S(1)} %pad_convert_fusion.refs_6_), channel_id=1, source_target_pairs={{0,1},{1,0},{2,3},{3,2},{4,5},{5,4},{6,7},{7,6},{8,9},{9,8},{10,11... | collective-permute-start | bytes 36872 | tf_op jit(solution)/shard_map/ppermute | solution.py:1073
  14.2 17.6 %collective-permute-start.1 = (bf16[192,1152]{1,0:T(8,128)(2,1)S(1)}, bf16[192,1152]{1,0:T(8,128)(2,1)S(1)}, u32[]{:S(2)}, u32[]{:S(2)}) collective-permute-start(bf16[192,1152]{1,0:T(8,128)(2,1)S(1)} %constant_dynamic-slice_fusion.3), channel_id=1, source_target_pairs={{0,1},{1,0},{2,3},{3,2},{4,5},{5,4},{6,7},{7,6},{8,9},{9,8},{10,11... | collective-permute-start | bytes 1327112 | tf_op jit(solution)/shard_map/ppermute | solution.py:1073
  16.2 15.5 %collective-permute-start.2 = (bf16[384,384]{1,0:T(8,128)(2,1)S(1)}, bf16[384,384]{1,0:T(8,128)(2,1)}, u32[]{:S(2)}, u32[]{:S(2)}) collective-permute-start(bf16[384,384]{1,0:T(8,128)(2,1)S(1)} %constant_dynamic-slice_fusion.2), channel_id=1, source_target_pairs={{0,1},{1,0},{2,3},{3,2},{4,5},{5,4},{6,7},{7,6},{8,9},{9,8},{10,11... | collective-permute-start | bytes 884744 | tf_op jit(solution)/shard_map/ppermute | solution.py:1073
  31.8 17.6 %collective-permute-start.7 = (bf16[768,384]{1,0:T(8,128)(2,1)S(1)}, bf16[768,384]{1,0:T(8,128)(2,1)S(1)}, u32[]{:S(2)}, u32[]{:S(2)}) collective-permute-start(bf16[768,384]{1,0:T(8,128)(2,1)S(1)} %constant_dynamic-slice_fusion.1), channel_id=1, source_target_pairs={{0,1},{1,0},{2,3},{3,2},{4,5},{5,4},{6,7},{7,6},{8,9},{9,8},{10,11... | collective-permute-start | bytes 1769480 | tf_op jit(solution)/shard_map/ppermute | solution.py:1073
  34.9 14.5 %collective-permute-start.6 = (bf16[192,1152]{1,0:T(8,128)(2,1)S(1)}, bf16[192,1152]{1,0:T(8,128)(2,1)S(1)}, u32[]{:S(2)}, u32[]{:S(2)}) collective-permute-start(bf16[192,1152]{1,0:T(8,128)(2,1)S(1)} %collective-permute-done.1), channel_id=1, source_target_pairs={{0,4},{4,0},{1,5},{5,1},{2,6},{6,2},{3,7},{7,3},{8,12},{12,8},{9,1... | collective-permute-start | bytes 1327112 | tf_op jit(solution)/shard_map/ppermute | solution.py:1073
  49.7 25.2 %collective-permute-start.11 = (bf16[768,768]{1,0:T(8,128)(2,1)S(1)}, bf16[768,768]{1,0:T(8,128)(2,1)}, u32[]{:S(2)}, u32[]{:S(2)}) collective-permute-start(bf16[768,768]{1,0:T(8,128)(2,1)S(1)} %constant_dynamic-slice_fusion), channel_id=1, source_target_pairs={{0,1},{1,0},{2,3},{3,2},{4,5},{5,4},{6,7},{7,6},{8,9},{9,8},{10,11... | collective-permute-start | bytes 3538952 | tf_op jit(solution)/shard_map/ppermute | solution.py:1073
  50.3 22.0 %collective-permute-start.10 = (bf16[768,384]{1,0:T(8,128)(2,1)S(1)}, bf16[768,384]{1,0:T(8,128)(2,1)}, u32[]{:S(2)}, u32[]{:S(2)}) collective-permute-start(bf16[768,384]{1,0:T(8,128)(2,1)S(1)} %collective-permute-done.7), channel_id=1, source_target_pairs={{0,4},{4,0},{1,5},{5,1},{2,6},{6,2},{3,7},{7,3},{8,12},{12,8},{9,1... | collective-permute-start | bytes 1769480 | tf_op jit(solution)/shard_map/ppermute | solution.py:1073
  76.4 22.3 %collective-permute-start.12 = (bf16[768,768]{1,0:T(8,128)(2,1)S(1)}, bf16[768,768]{1,0:T(8,128)(2,1)}, u32[]{:S(2)}, u32[]{:S(2)}) collective-permute-start(bf16[768,768]{1,0:T(8,128)(2,1)S(1)} %maximum_select_fusion.rest_0_), channel_id=1, source_target_pairs={{0,2},{2,0},{1,3},{3,1},{4,6},{6,4},{5,7},{7,5},{8,10},{10,8},{9,1... | collective-permute-start | bytes 3538952 | tf_op jit(solution)/shard_map/ppermute | solution.py:1073
  76.5 22.2 %collective-permute-start.13 = (bf16[768,768]{1,0:T(8,128)(2,1)}, bf16[768,768]{1,0:T(8,128)(2,1)}, u32[]{:S(2)}, u32[]{:S(2)}) collective-permute-start(bf16[768,768]{1,0:T(8,128)(2,1)} %collective-permute-done.11.rest_2_), channel_id=1, source_target_pairs={{0,2},{2,0},{1,3},{3,1},{4,6},{6,4},{5,7},{7,5},{8,10},{10,8},{9,1... | collective-permute-start | bytes 3538952 | tf_op jit(solution)/shard_map/ppermute | solution.py:1073
  98.6 22.5 %collective-permute-start.14 = (bf16[2,1536,384]{2,1,0:T(8,128)(2,1)}, bf16[2,1536,384]{2,1,0:T(8,128)(2,1)S(1)}, u32[]{:S(2)}, u32[]{:S(2)}) collective-permute-start(bf16[2,1536,384]{2,1,0:T(8,128)(2,1)} %get-tuple-element.186), channel_id=1, source_target_pairs={{0,2},{2,0},{1,3},{3,1},{4,6},{6,4},{5,7},{7,5},{8,10},{10,8},{9,1... | collective-permute-start | bytes 7077896 | tf_op jit(solution)/shard_map/ppermute | solution.py:1073
  128.5 28.5 %collective-permute-start.17 = (bf16[2,768,384]{2,1,0:T(8,128)(2,1)}, bf16[2,768,384]{2,1,0:T(8,128)(2,1)}, u32[]{:S(2)}, u32[]{:S(2)}) collective-permute-start(bf16[2,768,384]{2,1,0:T(8,128)(2,1)} %pad_maximum_fusion.1), channel_id=1, source_target_pairs={{0,4},{4,0},{1,5},{5,1},{2,6},{6,2},{3,7},{7,3},{8,12},{12,8},{9,1... | collective-permute-start | bytes 3538952 | tf_op jit(solution)/shard_map/ppermute | solution.py:1073
  129.1 28.2 %collective-permute-start.16 = (bf16[2,768,384]{2,1,0:T(8,128)(2,1)}, bf16[2,768,384]{2,1,0:T(8,128)(2,1)}, u32[]{:S(2)}, u32[]{:S(2)}) collective-permute-start(bf16[2,768,384]{2,1,0:T(8,128)(2,1)} %get-tuple-element.189), channel_id=1, source_target_pairs={{0,1},{1,0},{2,3},{3,2},{4,5},{5,4},{6,7},{7,6},{8,9},{9,8},{10,11... | collective-permute-start | bytes 3538952 | tf_op jit(solution)/shard_map/ppermute | solution.py:1073
  157.3 27.0 %collective-permute-start.18 = (bf16[2,768,384]{2,1,0:T(8,128)(2,1)}, bf16[2,768,384]{2,1,0:T(8,128)(2,1)}, u32[]{:S(2)}, u32[]{:S(2)}) collective-permute-start(bf16[2,768,384]{2,1,0:T(8,128)(2,1)} %get-tuple-element.202), channel_id=1, source_target_pairs={{0,2},{2,0},{1,3},{3,1},{4,6},{6,4},{5,7},{7,5},{8,10},{10,8},{9,1... | collective-permute-start | bytes 3538952 | tf_op jit(solution)/shard_map/ppermute | solution.py:1073
  159.3 24.9 %collective-permute-start.20 = (bf16[768,384]{1,0:T(8,128)(2,1)}, bf16[768,384]{1,0:T(8,128)(2,1)}, u32[]{:S(2)}, u32[]{:S(2)}) collective-permute-start(bf16[768,384]{1,0:T(8,128)(2,1)} %fusion.3), channel_id=1, source_target_pairs={{0,4},{4,0},{1,5},{5,1},{2,6},{6,2},{3,7},{7,3},{8,12},{12,8},{9,1... | collective-permute-start | bytes 1769480 | tf_op jit(solution)/shard_map/ppermute | solution.py:1073
  162.7 21.5 %collective-permute-start.19 = (bf16[768,384]{1,0:T(8,128)(2,1)}, bf16[768,384]{1,0:T(8,128)(2,1)S(1)}, u32[]{:S(2)}, u32[]{:S(2)}) collective-permute-start(bf16[768,384]{1,0:T(8,128)(2,1)} %fusion.2), channel_id=1, source_target_pairs={{0,1},{1,0},{2,3},{3,2},{4,5},{5,4},{6,7},{7,6},{8,9},{9,8},{10,11... | collective-permute-start | bytes 1769480 | tf_op jit(solution)/shard_map/ppermute | solution.py:1073
  184.3 9.0 %collective-permute-start.21 = (bf16[2,768,384]{2,1,0:T(8,128)(2,1)}, bf16[2,768,384]{2,1,0:T(8,128)(2,1)}, u32[]{:S(2)}, u32[]{:S(2)}) collective-permute-start(bf16[2,768,384]{2,1,0:T(8,128)(2,1)} %get-tuple-element.208), channel_id=1, source_target_pairs={{0,2},{2,0},{1,3},{3,1},{4,6},{6,4},{5,7},{7,5},{8,10},{10,8},{9,1... | collective-permute-start | bytes 3538952 | tf_op jit(solution)/shard_map/ppermute | solution.py:1073
  187.2 22.5 %collective-permute-start.22 = (bf16[2,384,384]{2,1,0:T(8,128)(2,1)}, bf16[2,384,384]{2,1,0:T(8,128)(2,1)}, u32[]{:S(2)}, u32[]{:S(2)}) collective-permute-start(bf16[2,384,384]{2,1,0:T(8,128)(2,1)} %get-tuple-element.294), channel_id=1, source_target_pairs={{0,1},{1,0},{2,3},{3,2},{4,5},{5,4},{6,7},{7,6},{8,9},{9,8},{10,11... | collective-permute-start | bytes 1769480 | tf_op jit(solution)/shard_map/ppermute | solution.py:1073
  191.7 18.0 %collective-permute-start.24 = (bf16[768,384]{1,0:T(8,128)(2,1)}, bf16[768,384]{1,0:T(8,128)(2,1)S(1)}, u32[]{:S(2)}, u32[]{:S(2)}) collective-permute-start(bf16[768,384]{1,0:T(8,128)(2,1)} %get-tuple-element.286), channel_id=1, source_target_pairs={{0,8},{8,0},{16,24},{24,16},{1,9},{9,1},{17,25},{25,17},{2,10},{10... | collective-permute-start | bytes 1769480 | tf_op jit(solution)/shard_map/ppermute | solution.py:1073
  195.7 15.2 %collective-permute-start.23 = (bf16[2,384,384]{2,1,0:T(8,128)(2,1)}, bf16[2,384,384]{2,1,0:T(8,128)(2,1)S(1)}, u32[]{:S(2)}, u32[]{:S(2)}) collective-permute-start(bf16[2,384,384]{2,1,0:T(8,128)(2,1)} %pad_maximum_fusion.2), channel_id=1, source_target_pairs={{0,4},{4,0},{1,5},{5,1},{2,6},{6,2},{3,7},{7,3},{8,12},{12,8},{9,1... | collective-permute-start | bytes 1769480 | tf_op jit(solution)/shard_map/ppermute | solution.py:1073
  215.4 15.1 %collective-permute-start.25 = (bf16[384,384]{1,0:T(8,128)(2,1)S(1)}, bf16[384,384]{1,0:T(8,128)(2,1)S(1)}, u32[]{:S(2)}, u32[]{:S(2)}) collective-permute-start(bf16[384,384]{1,0:T(8,128)(2,1)S(1)} %get-tuple-element.298), channel_id=1, source_target_pairs={{0,16},{8,24},{16,0},{24,8},{1,17},{9,25},{17,1},{25,9},{2,18},{10... | collective-permute-start | bytes 884744 | tf_op jit(solution)/shard_map/ppermute | solution.py:1073
  233.1 13.8 %collective-permute-start.28 = (bf16[384,384]{1,0:T(8,128)(2,1)S(1)}, bf16[384,384]{1,0:T(8,128)(2,1)S(1)}, u32[]{:S(2)}, u32[]{:S(2)}) collective-permute-start(bf16[384,384]{1,0:T(8,128)(2,1)S(1)} %get-tuple-element.295), channel_id=1, source_target_pairs={{0,8},{8,0},{16,24},{24,16},{1,9},{9,1},{17,25},{25,17},{2,10},{10... | collective-permute-start | bytes 884744 | tf_op jit(solution)/shard_map/ppermute | solution.py:1073
  233.2 16.0 %collective-permute-start.30 = (bf16[384,384]{1,0:T(8,128)(2,1)S(1)}, bf16[384,384]{1,0:T(8,128)(2,1)S(1)}, u32[]{:S(2)}, u32[]{:S(2)}) collective-permute-start(bf16[384,384]{1,0:T(8,128)(2,1)S(1)} %add_convert_fusion.12), channel_id=1, source_target_pairs={{0,16},{8,24},{16,0},{24,8},{1,17},{9,25},{17,1},{25,9},{2,18},{10... | collective-permute-start | bytes 884744 | tf_op jit(solution)/shard_map/ppermute | solution.py:1073
  247.0 10.1 %collective-permute-start.31 = (bf16[192,384]{1,0:T(8,128)(2,1)S(1)}, bf16[192,384]{1,0:T(8,128)(2,1)S(1)}, u32[]{:S(2)}, u32[]{:S(2)}) collective-permute-start(bf16[192,384]{1,0:T(8,128)(2,1)S(1)} %get-tuple-element.301), channel_id=1, source_target_pairs={{0,16},{8,24},{16,0},{24,8},{1,17},{9,25},{17,1},{25,9},{2,18},{10... | collective-permute-start | bytes 442376 | tf_op jit(solution)/shard_map/ppermute | solution.py:1073
  259.2 16.4 %collective-permute-start.35 = (bf16[2,384,384]{2,1,0:T(8,128)(2,1)S(1)}, bf16[2,384,384]{2,1,0:T(8,128)(2,1)S(1)}, u32[]{:S(2)}, u32[]{:S(2)}) collective-permute-start(bf16[2,384,384]{2,1,0:T(8,128)(2,1)S(1)} %pad_maximum_fusion.3), channel_id=1, source_target_pairs={{0,8},{8,0},{16,24},{24,16},{1,9},{9,1},{17,25},{25,17},{2,10},{10... | collective-permute-start | bytes 1769480 | tf_op jit(solution)/shard_map/ppermute | solution.py:1073
  264.4 11.2 %collective-permute-start.36 = (bf16[24,1536]{1,0:T(8,128)(2,1)S(1)}, bf16[24,1536]{1,0:T(8,128)(2,1)S(1)}, u32[]{:S(2)}, u32[]{:S(2)}) collective-permute-start(bf16[24,1536]{1,0:T(8,128)(2,1)S(1)} %add_convert_fusion.26), channel_id=1, source_target_pairs={{0,8},{8,0},{16,24},{24,16},{1,9},{9,1},{17,25},{25,17},{2,10},{10... | collective-permute-start | bytes 221192 | tf_op jit(solution)/shard_map/ppermute | solution.py:1073
  275.7 12.9 %collective-permute-start.38 = (bf16[24,1536]{1,0:T(8,128)(2,1)S(1)}, bf16[24,1536]{1,0:T(8,128)(2,1)S(1)}, u32[]{:S(2)}, u32[]{:S(2)}) collective-permute-start(bf16[24,1536]{1,0:T(8,128)(2,1)S(1)} %add_convert_fusion.25), channel_id=1, source_target_pairs={{0,16},{8,24},{16,0},{24,8},{1,17},{9,25},{17,1},{25,9},{2,18},{10... | collective-permute-start | bytes 221192 | tf_op jit(solution)/shard_map/ppermute | solution.py:1073
  276.3 31.6 %collective-permute-start.40 = (bf16[4,384,384]{2,1,0:T(8,128)(2,1)S(1)}, bf16[4,384,384]{2,1,0:T(8,128)(2,1)}, u32[]{:S(2)}, u32[]{:S(2)}) collective-permute-start(bf16[4,384,384]{2,1,0:T(8,128)(2,1)S(1)} %constant_dynamic-update-slice_fusion), channel_id=1, source_target_pairs={{0,4},{4,0},{1,5},{5,1},{2,6},{6,2},{3,7},{7,3},{8,12},{12,8},{9,1... | collective-permute-start | bytes 3538952 | tf_op jit(solution)/shard_map/ppermute | solution.py:1073
  277.0 16.6 %collective-permute-start.37 = (bf16[2,192,384]{2,1,0:T(8,128)(2,1)S(1)}, bf16[2,192,384]{2,1,0:T(8,128)(2,1)S(1)}, u32[]{:S(2)}, u32[]{:S(2)}) collective-permute-start(bf16[2,192,384]{2,1,0:T(8,128)(2,1)S(1)} %pad_maximum_fusion.5), channel_id=1, source_target_pairs={{0,16},{8,24},{16,0},{24,8},{1,17},{9,25},{17,1},{25,9},{2,18},{10... | collective-permute-start | bytes 884744 | tf_op jit(solution)/shard_map/ppermute | solution.py:1073
  293.7 14.1 %collective-permute-start.39 = (bf16[2,2,192,384]{3,2,1,0:T(8,128)(2,1)S(1)}, bf16[2,2,192,384]{3,2,1,0:T(8,128)(2,1)S(1)}, u32[]{:S(2)}, u32[]{:S(2)}) collective-permute-start(bf16[2,2,192,384]{3,2,1,0:T(8,128)(2,1)S(1)} %pad_maximum_fusion.4), channel_id=1, source_target_pairs={{0,8},{8,0},{16,24},{24,16},{1,9},{9,1},{17,25},{25,17},{2,10},{10... | collective-permute-start | bytes 1769480 | tf_op jit(solution)/shard_map/ppermute | solution.py:1073
  313.5 9.7 %collective-permute-start.42 = (bf16[2,4,384,384]{3,2,1,0:T(8,128)(2,1)S(1)}, bf16[2,4,384,384]{3,2,1,0:T(8,128)(2,1)}, u32[]{:S(2)}, u32[]{:S(2)}) collective-permute-start(bf16[2,4,384,384]{3,2,1,0:T(8,128)(2,1)S(1)} %pad_maximum_fusion.a.b), channel_id=1, source_target_pairs={{0,2},{2,0},{1,3},{3,1},{4,6},{6,4},{5,7},{7,5},{8,10},{10,8},{9,1... | collective-permute-start | bytes 7077896 | tf_op jit(solution)/shard_map/ppermute | solution.py:1073
  (46 other events, 247.1 us)
where the time goes:
time: 336 us; the launch traced here: 332 us
  Pallas kernels  170 us (51%)
  waiting for transfers between devices  78.8 us (23%)
  starting transfers between devices  35.6 us (11%)
  other arithmetic  30.5 us (9%)
  local copies, waits for them, and re-layouts  15.3 us (5%)
    pallas_call x9, Pallas kernels, call(): return f(self.meta, *[a for a, _ in ins])  149 us
    ppermute x43, waiting for transfers between devices, swap(): return lax.ppermute(a, axis, [(i, i ^ step) for i in range(n)])  78.8 us
    ppermute x43, starting transfers between devices, swap(): return lax.ppermute(a, axis, [(i, i ^ step) for i in range(n)])  35.6 us
    convert_element_type x17, other arithmetic, plus(): return total.astype(BF)  16.9 us
    pallas_call x1, Pallas kernels, place_feed(): pl.pallas_call(place_feed_kernel, grid_spec=pltpu.PrefetchScalarGridSpec(...  8.77 us
  transfers between devices with their start and end apart: 43, of which 20 were waited for; matrix products, arithmetic and copies ran while one was open for 10% of the time, Pallas kernels for 49%

commit v1 on v0

--- a/solution.py
+++ b/solution.py
@@ -269,6 +269,14 @@
     return out
 
 
+def run_copies(pairs, sem):
+    copies = [pltpu.make_async_copy(x, y, sem.at[i]) for i, (x, y) in enumerate(pairs)]
+    for x in copies:
+        x.start()
+    for x in copies:
+        x.wait()
+
+
 def attend_kernel(pieces, groups, tail, prior, meta, live, first, perm, pick, mask, bias, rel, *rest):
     w, rest = rest[:pieces], rest[pieces:]
     if tail:
@@ -276,19 +284,41 @@
         before, rest = rest[:prior], rest[prior:]
         w_before, rest = rest[:prior], rest[prior:]
         w_out, rest = rest[:pieces], rest[pieces:]
-        qkv, probs, mixed_out, middle, second, table, mixed, att = rest
+    k = 3 + prior if tail else 2
+    sources, rest = rest[:k], rest[k:]
+    loaded = (live, first) + ((xc, *before) if tail else ())
+    if tail:
+        qkv_out, probs_out, mixed_out, middle_out, second_out, table, qkv, probs, mixed, in_sem, sem = rest[:11]
+        middle, second, att = rest[11:]
     else:
-        qkv, probs, mixed_out, table = rest
+        qkv_out, probs_out, mixed_out, table, qkv, probs, mixed, in_sem, sem = rest
     rows, d = first.shape
     blocks = rows // BLK
-    chunk, step = pl.program_id(0), pl.program_id(1)
+    step = pl.program_id(0)
+    chunks = meta[2]
     c = meta[AT_C]
     n0 = meta[1]
     near = pl.ds(pl.multiple_of(c * (d // 2), BLK), d // 2)
     far = pl.ds(pl.multiple_of((1 - c) * (d // 2), BLK), d // 2)
-
-    @pl.when(step < groups)
-    def _():
+    last = groups if tail else groups - 1
+
+    def reload(chunk):
+        @pl.when(chunks > 1)
+        def _():
+            at = pl.ds(pl.multiple_of(chunk * rows, rows), rows)
+            run_copies([(x.at[at, :], y) for x, y in zip(sources, loaded)], in_sem)
+
+    def stores(chunk, g):
+        at = pl.ds(pl.multiple_of(chunk * rows, rows), rows)
+        cols = pl.ds(pl.multiple_of(g * GW, BLK), GW)
+        return (
+            pltpu.make_async_copy(qkv, qkv_out.at[at, cols], sem.at[0]),
+            pltpu.make_async_copy(probs, probs_out.at[pl.ds(chunk * blocks, blocks), g], sem.at[1]),
+        )
+
+    def group(i, carry):
+        chunk = chunks - 1 - i
+        reload(chunk)
         if pieces == 1:
             v = dot(first[...], w[0][...])
         else:
@@ -296,21 +326,17 @@
         v = v + bias[...]
         block = lax.broadcasted_iota(jnp.int32, (1, GW), 1) >> 5
         is_q = block == 0
-        for i in range(3, 3 * GROUP, 3):
-            is_q = is_q | (block == i)
+        for j in range(3, 3 * GROUP, 3):
+            is_q = is_q | (block == j)
         v = (v * jnp.where(is_q, HEAD_DIM**-0.5, 1.0)).astype(BF)
+
+        @pl.when((step > 0) | (i > 0))
+        def _():
+            for x in stores(0, 0):
+                x.wait()
+
         qkv[...] = dot(v, perm[...]).astype(BF)
-        places = []
-        for h in range(GROUP):
-            row = rel[pl.ds(step * GROUP + h, 1), :]
-            row = pltpu.roll(jnp.broadcast_to(row, (BLK, 2 * BLK)), 2 * BLK - 88, 1, stride=1, stride_axis=0)
-            places.append(row[:, 0:BLK].astype(BF))
-        for kind in range(2):
-            e = pick[kind]
-            for h in range(GROUP):
-                half = dot(e, places[h]).astype(BF)
-                t = dot_nt(half, e) + mask[kind].astype(F32)
-                table[kind, h * BLK : (h + 1) * BLK, :] = t.astype(BF)
+        stores(chunk, step)[0].start()
         for b in range(blocks):
             at = slice(b * BLK, (b + 1) * BLK)
             kind = jnp.where(chunk * blocks + b < n0, 0, 1)
@@ -324,23 +350,36 @@
             e = jnp.exp(st - peak)
             p = (e * (1.0 / jnp.sum(e, axis=1, keepdims=True))).astype(BF)
             p = p.reshape(GROUP * BLK, BLK)
-            probs[b, 0] = p
+            probs[b] = p
             vt = v.astype(F32).T.astype(BF)
             m = dot(spread_cols(vt), p).T.astype(BF)
-            mixed_out[at, :] = m
-            if tail:
-                mixed[at, pl.ds(pl.multiple_of(step * BLK, BLK), BLK)] = m
-
-    if not tail:
-        return
-
-    @pl.when(step == groups)
+            mixed[chunk, at, pl.ds(pl.multiple_of(step * BLK, BLK), BLK)] = m
+        stores(chunk, step)[1].start()
+        return carry
+
+    @pl.when(step < groups)
     def _():
+        places = []
+        for h in range(GROUP):
+            row = rel[pl.ds(step * GROUP + h, 1), :]
+            row = pltpu.roll(jnp.broadcast_to(row, (BLK, 2 * BLK)), 2 * BLK - 88, 1, stride=1, stride_axis=0)
+            places.append(row[:, 0:BLK].astype(BF))
+        for kind in range(2):
+            e = pick[kind]
+            for h in range(GROUP):
+                half = dot(e, places[h]).astype(BF)
+                t = dot_nt(half, e) + mask[kind].astype(F32)
+                table[kind, h * BLK : (h + 1) * BLK, :] = t.astype(BF)
+        lax.fori_loop(0, chunks, group, 0)
+
+    def project(i, carry):
+        chunk = chunks - 1 - i
+        reload(chunk)
         if pieces == 1:
-            att[...] = dot(mixed[...], w_out[0][...])
+            att[...] = dot(mixed[chunk], w_out[0][...])
         else:
-            att[:, near] = dot(mixed[...], w_out[0][...])
-            att[:, far] = dot(mixed[...], w_out[1][...])
+            att[:, near] = dot(mixed[chunk], w_out[0][...])
+            att[:, far] = dot(mixed[chunk], w_out[1][...])
         for m, v in zip(before, w_before):
             att[...] = att[...] + dot(m[...], v[...])
         for b in range(blocks):
@@ -349,6 +388,31 @@
             middle[at, :] = m
             nrm, _ = norm_stats(m)
             second[at, :] = (nrm * vecs[G2] + vecs[B2]).astype(BF)
+        at = pl.ds(pl.multiple_of(chunk * rows, rows), rows)
+        run_copies([(middle, middle_out.at[at, :]), (second, second_out.at[at, :])], in_sem)
+        return carry
+
+    def give(chunk):
+        at = pl.ds(pl.multiple_of(chunk * rows, rows), rows)
+        return pltpu.make_async_copy(mixed.at[chunk], mixed_out.at[at, :], sem.at[2])
+
+    if tail:
+
+        @pl.when(step == groups)
+        def _():
+            lax.fori_loop(0, chunks, project, 0)
+
+    @pl.when(step == last)
+    def _():
+        for x in stores(0, 0):
+            x.wait()
+
+        def out(i, carry):
+            give(i).start()
+            give(i).wait()
+            return carry
+
+        lax.fori_loop(0, chunks, out, 0)
 
 
 def feed_kernel(tiles, pieces, last, prior, meta, second, branch, *rest):
@@ -523,51 +587,67 @@
 
 def back_kernel(pieces, groups, split, meta, ag, perm, pick, pick_t, qkv, probs, mixed, first, *rest):
     w_out, rest = rest[:pieces], rest[pieces:]
+    sources, rest = rest[:5], rest[5:]
     dqkv, rest = rest[0], rest[1:]
     grads, rest = rest[: 2 if split else 1], rest[2 if split else 1 :]
-    dba, drel, dperm, dmix, table = rest
+    dba, drel, dperm, dmix, table, out, in_sem, sem = rest
     rows, d = ag.shape
     blocks = rows // BLK
-    step, chunk = pl.program_id(0), pl.program_id(1)
+    step = pl.program_id(0)
+    chunks = meta[2]
     n0 = meta[1]
     c, me = meta[AT_C], meta[AT_ME]
     half = d // 2
     stays = (step >> 1) == (me >> 1)
 
-    def put(ref, value):
-        @pl.when(chunk == 0)
+    def reload(chunk):
+        @pl.when(chunks > 1)
+        def _():
+            at = pl.ds(pl.multiple_of(chunk * rows, rows), rows)
+            g = jnp.minimum(step, groups - 1)
+            cols = pl.ds(pl.multiple_of(g * GW, BLK), GW)
+            ag_h, qkv_h, probs_h, mixed_h, first_h = sources
+            pairs = [(ag_h.at[at, :], ag), (qkv_h.at[at, cols], qkv), (mixed_h.at[at, :], mixed), (first_h.at[at, :], first)]
+            pairs += [(probs_h.at[pl.ds(chunk * blocks, blocks), g], probs.at[:, 0])]
+            run_copies(pairs, in_sem)
+
+    def store(chunk, g):
+        at = pl.ds(pl.multiple_of(chunk * rows, rows), rows)
+        cols = pl.ds(pl.multiple_of(g * GW, BLK), GW)
+        return pltpu.make_async_copy(out, dqkv.at[at, cols], sem.at[0])
+
+    def put(i, ref, value):
+        @pl.when(i == 0)
         def _():
             ref[...] = value.astype(ref.dtype)
 
-        @pl.when(chunk > 0)
+        @pl.when(i > 0)
         def _():
             ref[...] = (ref[...].astype(F32) + value).astype(ref.dtype)
 
-    def put_grad(low, high, value):
+    def put_grad(i, low, high, value):
         if not split:
-            put(grads[0].at[0, low:high, :], value)
+            put(i, grads[0].at[0, low:high, :], value)
             return
 
         @pl.when(stays)
         def _():
-            put(grads[0].at[0, low:high, :], value)
+            put(i, grads[0].at[0, low:high, :], value)
 
         @pl.when(jnp.logical_not(stays))
         def _():
-            put(grads[1].at[0, low:high, :], value)
-
-    @pl.when(step == groups)
-    def _():
+            put(i, grads[1].at[0, low:high, :], value)
+
+    def weights(i, carry):
+        reload(chunks - 1 - i)
         wide = groups * BLK
-        for i in range(2):
-            put_grad(i * wide, (i + 1) * wide, dot_tn(mixed[...], ag[:, i * half : (i + 1) * half]))
-
-    @pl.when(step < groups)
-    def _():
-        @pl.when(chunk == 0)
-        def _():
-            table[...] = jnp.zeros_like(table)
-
+        for j in range(2):
+            put_grad(i, j * wide, (j + 1) * wide, dot_tn(mixed[...], ag[:, j * half : (j + 1) * half]))
+        return carry
+
+    def heads(i, carry):
+        chunk = chunks - 1 - i
+        reload(chunk)
         if pieces == 1:
             dmix[...] = dot_nt(ag[...], w_out[0][...]).astype(BF)
         else:
@@ -596,36 +676,49 @@
             dperm[at, BLK : 2 * BLK] = dk.astype(BF)
             dperm[at, 2 * BLK : 3 * BLK] = dv.astype(BF)
         x = dot_nt(dperm[...], perm[...]).astype(BF)
-        dqkv[...] = x
-        put_grad(0, d, dot_tn(first[...], x))
-        put(dba, jnp.sum(x.astype(F32), axis=0, keepdims=True))
-
-        @pl.when(chunk == meta[2] - 1)
-        def _():
-            for h in range(GROUP):
-                total = jnp.zeros((BLK, BLK), F32)
-                for kind in range(2):
-                    a = table[kind, h * BLK : (h + 1) * BLK, :]
-                    a = dot(a.astype(BF), pick[kind]).astype(BF)
-                    total = total + dot(pick_t[kind], a)
-                wide = jnp.concatenate([total, jnp.zeros_like(total)], axis=1)
-                wide = pltpu.roll(wide, 0, 1, stride=1, stride_axis=0)
-                drel[pl.ds(step * GROUP + h, 1), :] = jnp.sum(wide, axis=0, keepdims=True)
+
+        @pl.when((step > 0) | (i > 0))
+        def _():
+            store(0, 0).wait()
+
+        out[...] = x
+        store(chunk, step).start()
+        put_grad(i, 0, d, dot_tn(first[...], x))
+        put(i, dba, jnp.sum(x.astype(F32), axis=0, keepdims=True))
+        return carry
+
+    @pl.when(step == groups)
+    def _():
+        lax.fori_loop(0, chunks, weights, 0)
+        store(0, 0).wait()
+
+    @pl.when(step < groups)
+    def _():
+        table[...] = jnp.zeros_like(table)
+        lax.fori_loop(0, chunks, heads, 0)
+        for h in range(GROUP):
+            total = jnp.zeros((BLK, BLK), F32)
+            for kind in range(2):
+                a = table[kind, h * BLK : (h + 1) * BLK, :]
+                a = dot(a.astype(BF), pick[kind]).astype(BF)
+                total = total + dot(pick_t[kind], a)
+            wide = jnp.concatenate([total, jnp.zeros_like(total)], axis=1)
+            wide = pltpu.roll(wide, 0, 1, stride=1, stride_axis=0)
+            drel[pl.ds(step * GROUP + h, 1), :] = jnp.sum(wide, axis=0, keepdims=True)
 
 
 def row_tiles(rows, size=384):
     return [(a, min(size, rows - a)) for a in range(0, rows, size)]
 
 
-def ends_kernel(pieces, meta, live, xc, cotc, middle, mg, vecs, *rest):
+def ends_kernel(pieces, meta, live, xc, cotc, mg, vecs, *rest):
     n = len(pieces)
-    red, rest = rest[:n], rest[n:]
     dqkv, rest = rest[:n], rest[n:]
     w = []
     for k in pieces:
         w.append(rest[:k])
         rest = rest[k:]
-    res, hi, lo, vec, fg = rest
+    hi, lo, vec, fg = rest
     rows, d = xc.shape
     blocks = rows // BLK
     chunk = pl.program_id(0)
@@ -655,35 +748,52 @@
         top = delta.astype(BF)
         hi[at, :] = top
         lo[at, :] = (delta - top.astype(F32)).astype(BF)
+        vec[0:1, :] = vec[0:1, :] + jnp.sum(g * nrm, axis=0, keepdims=True)
+        vec[1:2, :] = vec[1:2, :] + jnp.sum(g, axis=0, keepdims=True)
+        vec[2:3, :] = vec[2:3, :] + jnp.sum(up * keep, axis=0, keepdims=True)
+
+
+def result_kernel(prior, meta, idx, live, middle, vecs, patches, *rest):
+    red, (result, res) = rest[:prior], rest[prior:]
+    rows = middle.shape[0]
+    chunk = pl.program_id(0)
+    for b in range(rows // BLK):
+        at = slice(b * BLK, (b + 1) * BLK)
         reduced = vecs[RB]
         for x in red:
             reduced = reduced + x[at, :].astype(F32)
-        res[at, :] = (middle[at, :] + keep * reduced).astype(BF)
-        vec[0:1, :] = vec[0:1, :] + jnp.sum(g * nrm, axis=0, keepdims=True)
-        vec[1:2, :] = vec[1:2, :] + jnp.sum(g, axis=0, keepdims=True)
-        vec[2:3, :] = vec[2:3, :] + jnp.sum(up * keep, axis=0, keepdims=True)
-
-
-def scatter_kernel(meta, idx, res, hi, lo, patches, cot, result, input_grad):
-    rows = res.shape[0]
-    chunk = pl.program_id(0)
+        res[at, :] = (middle[at, :] + live[at, :] * reduced).astype(BF)
     for start, size in row_tiles(patches.shape[0]):
         at = slice(start, start + size)
         spots = start + lax.broadcasted_iota(jnp.int32, (size, rows), 0)
         hit = (spots == idx[0]).astype(F32)
         here = jnp.sum(hit, axis=1, keepdims=True) > 0.0
-        put = hit.astype(BF)
-        new = dot(put, res[...])
+        new = dot(hit.astype(BF), res[...])
+
+        @pl.when(chunk == 0)
+        def _():
+            result[at, :] = jnp.where(here, new, patches[at, :].astype(F32)).astype(BF)
+
+        @pl.when(chunk > 0)
+        def _():
+            result[at, :] = jnp.where(here, new, result[at, :].astype(F32)).astype(BF)
+
+
+def scatter_kernel(meta, idx, hi, lo, cot, input_grad):
+    rows = hi.shape[0]
+    chunk = pl.program_id(0)
+    for start, size in row_tiles(cot.shape[0]):
+        at = slice(start, start + size)
+        spots = start + lax.broadcasted_iota(jnp.int32, (size, rows), 0)
+        put = (spots == idx[0]).astype(F32).astype(BF)
         grad = dot(put, hi[...]) + dot(put, lo[...])
 
         @pl.when(chunk == 0)
         def _():
-            result[at, :] = jnp.where(here, new, patches[at, :].astype(F32)).astype(BF)
             input_grad[at, :] = cot[at, :].astype(F32) + grad
 
         @pl.when(chunk > 0)
         def _():
-            result[at, :] = jnp.where(here, new, result[at, :].astype(F32)).astype(BF)
             input_grad[at, :] = input_grad[at, :] + grad
 
 
@@ -728,41 +838,36 @@
     return 2 * (r & 1) + (r >> 1)
 
 
-def place_feed_kernel(ids, a, b, c, e, exp, red):
-    @pl.when(pl.program_id(0) < 4)
-    def _():
-        exp[...] = a[0, 0].astype(F32)
-        red[...] = b[0, 0].astype(F32).T
-
-    @pl.when(pl.program_id(0) >= 4)
-    def _():
-        exp[...] = c[0, 0].astype(F32)
-        red[...] = e[0, 0].astype(F32).T
-
-
-def place_feed(ids, near, far, d, hidden):
-    def spec(which, odd):
-        def at(j, ids):
-            j = jnp.minimum(j, 3) if which == 0 else jnp.maximum(j, 4)
-            return ((j >> 1) & 1) ^ ids[1], relative_z(2 * (j & 1) + odd, ids), 0, 0
-
-        return pl.BlockSpec((1, 1, GW, GW), at)
-
-    tile = lambda j, ids: ((j >> 2) ^ ids[0]) * 2 + ((j >> 1) & 1)
+def place_feed_kernel(ids, a, b, *rest):
+    exp, red = rest[-2:]
+    exp[...] = a[0, 0].astype(F32)
+    red[...] = b[0, 0].astype(F32).T
+
+
+def place_feed(ids, x, d, hidden, onto=()):
+    other = 1 if onto else 0
+
+    def spec(odd):
+        return pl.BlockSpec(
+            (1, 1, GW, GW), lambda j, ids: ((j >> 1) ^ ids[1], relative_z(2 * (j & 1) + odd, ids), 0, 0)
+        )
+
+    tile = lambda j, ids: (other ^ ids[0]) * 2 + (j >> 1)
     return pl.pallas_call(
         place_feed_kernel,
         grid_spec=pltpu.PrefetchScalarGridSpec(
             num_scalar_prefetch=1,
-            grid=(8,),
-            in_specs=[spec(0, 0), spec(0, 1), spec(1, 0), spec(1, 1)],
+            grid=(4,),
+            in_specs=[spec(0), spec(1)] + [ANY] * len(onto),
             out_specs=[
                 pl.BlockSpec((GW, GW), lambda j, ids: (j & 1, tile(j, ids))),
                 pl.BlockSpec((GW, GW), lambda j, ids: (tile(j, ids), j & 1)),
             ],
         ),
         out_shape=[sds((d, hidden), F32), sds((hidden, d), F32)],
+        input_output_aliases={3: 0, 4: 1} if onto else {},
         name="place_feed",
-    )(ids, near, near, far, far)
+    )(ids, x, x, *onto)
 
 
 def place_attend_kernel(ids, *refs):
@@ -913,37 +1018,36 @@
         ch, d = self.ch, first.shape[1]
         width = w[0].shape[1]
         groups = width // GW
-        clip = lambda i, g, meta: jnp.where(i < meta[2], jnp.minimum(g, groups - 1), groups - 1)
-        by_chunk = lambda a: (a, pl.BlockSpec((ch,) + a.shape[1:], lambda i, g, meta: (clamp(i, meta), 0)))
-        cols = lambda a, k: (a, pl.BlockSpec((a.shape[0], k), lambda i, g, meta: (0, clip(i, g, meta))))
-        out = lambda total, k, dt: (
-            sds((self.all, total), dt),
-            pl.BlockSpec((ch, k), lambda i, g, meta: (clamp(i, meta), clip(i, g, meta))),
-        )
+        clip = lambda g: jnp.minimum(g, groups - 1)
+        block = lambda a: (a, pl.BlockSpec((ch,) + a.shape[1:], lambda g, meta: (0, 0), pipeline_mode=pl.Buffered(1)))
+        cols = lambda a, k: (a, pl.BlockSpec((a.shape[0], k), lambda g, meta: (0, clip(g))))
+        full = lambda k, dt: (sds((self.all, k), dt), ANY)
         pshape = (self.per_chunk * self.chunks, groups, GROUP * BLK, BLK)
-        pspec = pl.BlockSpec((self.per_chunk, 1) + pshape[2:], lambda i, g, meta: (clamp(i, meta), clip(i, g, meta), 0, 0))
-        ins = [by_chunk(live), by_chunk(first), w_(self.perm), w_(self.up), w_(self.mask), cols(bias, GW), w_(rel)]
+        ins = [block(live), block(first), w_(self.perm), w_(self.up), w_(self.mask), cols(bias, GW), w_(rel)]
         ins += [cols(a, GW) for a in w]
-        outs = [out(width, GW, BF), (sds(pshape, BF), pspec), out(groups * BLK, BLK, BF)]
-        scratch = [pltpu.VMEM((2, GROUP * BLK, BLK), BF)]
+        outs = [full(width, BF), (sds(pshape, BF), ANY), full(groups * BLK, BF)]
+        v, dma = pltpu.VMEM, pltpu.SemaphoreType.DMA
+        scratch = [v((2, GROUP * BLK, BLK), BF), v((ch, GW), BF), v((self.per_chunk, GROUP * BLK, BLK), BF)]
+        scratch += [v((self.chunks, ch, groups * BLK), BF), dma((4,)), dma((3,))]
         steps = groups
+        again = [live, first]
         if tail is not None:
             steps += 1
             xc, vecs, wo = tail
-            ins += [by_chunk(xc), w_(vecs)]
-            ins += [by_chunk(m) for m, _ in before] + [w_(a) for _, a in before] + [w_(a) for a in wo]
-            outs += [
-                (sds((self.all, d), dt), pl.BlockSpec((ch, d), lambda i, g, meta: (clamp(i, meta), 0)))
-                for dt in (F32, BF)
-            ]
-            scratch += [pltpu.VMEM((ch, groups * BLK), BF), pltpu.VMEM((ch, d), F32)]
+            ins += [block(xc), w_(vecs)]
+            ins += [block(m) for m, _ in before] + [w_(a) for _, a in before] + [w_(a) for a in wo]
+            again += [xc] + [m for m, _ in before]
+            outs += [full(d, F32), full(d, BF)]
+            scratch += [v((ch, d), F32), v((ch, d), BF), v((ch, d), F32)]
+        ins += [(a, ANY) for a in again]
         return self.call(
             partial(attend_kernel, len(w), groups, tail is not None, len(before)),
             "attend",
             ins,
             outs,
             scratch,
-            grid=(self.chunks, steps),
+            grid=(steps,),
+            axis=None,
             flops=0.16 * ch * d * width,
             size=0.4 * ch * d,
         )
@@ -990,14 +1094,14 @@
         groups = width // GW
         split = groups == 3
         clip = lambda g: jnp.minimum(g, groups - 1)
-        by_chunk = lambda a: (a, pl.BlockSpec((ch,) + a.shape[1:], lambda g, i, meta: (clamp(i, meta), 0)))
-        cols = pl.BlockSpec((ch, GW), lambda g, i, meta: (clamp(i, meta), clip(g)))
-        pspec = pl.BlockSpec((self.per_chunk, 1) + probs.shape[2:], lambda g, i, meta: (clamp(i, meta), clip(g), 0, 0))
+        block = lambda a: (a, pl.BlockSpec((ch,) + a.shape[1:], lambda g, meta: (0, 0), pipeline_mode=pl.Buffered(1)))
+        cols = pl.BlockSpec((ch, GW), lambda g, meta: (0, clip(g)))
+        pspec = pl.BlockSpec((self.per_chunk, 1) + probs.shape[2:], lambda g, meta: (0, clip(g), 0, 0))
         one = (1, 2 * groups * BLK, GW)
         if split:
 
             def tile(start):
-                return lambda g, i, meta: (
+                return lambda g, meta: (
                     (jnp.clip(g - start(meta[AT_ME] >> 1), 0, 1) ^ meta[AT_ME]) & 1,
                     0,
                     0,
@@ -1006,50 +1110,66 @@
             shape = sds((2,) + one[1:], BF)
             grads = [(shape, pl.BlockSpec(one, tile(lambda h: 2 * h))), (shape, pl.BlockSpec(one, tile(lambda h: 2 - 2 * h)))]
         else:
-            grads = [(sds((groups + 1,) + one[1:], BF), pl.BlockSpec(one, lambda g, i, meta: (g, 0, 0)))]
-        rows = lambda a, k: pl.BlockSpec((k, a), lambda g, i, meta: (clip(g), 0))
+            grads = [(sds((groups + 1,) + one[1:], BF), pl.BlockSpec(one, lambda g, meta: (g, 0, 0)))]
+        v, dma = pltpu.VMEM, pltpu.SemaphoreType.DMA
         return self.call(
             partial(back_kernel, len(wo), groups, split),
             "back",
-            [by_chunk(ag), w_(self.perm), w_(self.up), w_(self.down_t), (qkv, cols), (probs, pspec)]
-            + [by_chunk(mixed), by_chunk(first)]
-            + [(a, rows(a.shape[1], BLK)) for a in wo],
-            [(sds((self.all, width), BF), cols), *grads]
-            + [(sds((1, width), F32), pl.BlockSpec((1, GW), lambda g, i, meta: (0, clip(g))))]
+            [block(ag), w_(self.perm), w_(self.up), w_(self.down_t), (qkv, cols), (probs, pspec)]
+            + [block(mixed), block(first)]
+            + [(a, pl.BlockSpec((BLK, a.shape[1]), lambda g, meta: (clip(g), 0))) for a in wo]
+            + [(a, ANY) for a in (ag, qkv, probs, mixed, first)],
+            [(sds((self.all, width), BF), ANY), *grads]
+            + [(sds((1, width), F32), pl.BlockSpec((1, GW), lambda g, meta: (0, clip(g))))]
             + [o_((groups * GROUP, 2 * BLK), F32)],
-            [pltpu.VMEM((ch, GW), BF), pltpu.VMEM((ch, BLK), BF), pltpu.VMEM((2, GROUP * BLK, BLK), F32)],
-            grid=(groups + 1, self.chunks),
-            axis=1,
+            [v((ch, GW), BF), v((ch, BLK), BF), v((2, GROUP * BLK, BLK), F32), v((ch, GW), BF), dma((5,)), dma((1,))],
+            grid=(groups + 1,),
+            axis=None,
             flops=14 * ch * d * width,
             size=30 * ch * d,
         )
 
-    def ends(self, live, xc, cotc, middle, mg, vecs, red, dqkv, ws):
+    def ends(self, live, xc, cotc, mg, vecs, dqkv, ws):
         ch, d = self.ch, xc.shape[1]
         c = self.c
         return self.call(
             partial(ends_kernel, [len(a) for a in ws]),
             "ends",
-            [c(live), c(xc), c(cotc), c(middle), c(mg), w_(vecs)]
-            + [c(a) for a in (*red, *dqkv)]
-            + [w_(a) for s in ws for a in s],
-            [self.row(d, BF)] * 3 + [o_((8, d), F32)],
+            [c(live), c(xc), c(cotc), c(mg), w_(vecs)] + [c(a) for a in dqkv] + [w_(a) for s in ws for a in s],
+            [self.row(d, BF)] * 2 + [o_((8, d), F32)],
             [pltpu.VMEM((ch, d), F32)],
             flops=6 * ch * d * d,
             size=30 * ch * d,
         )
 
-    def scatter(self, idx, res, hi, lo, patches, cot):
+    def by_row(self, idx):
+        return (idx, pl.BlockSpec((1, 1, self.ch), lambda i, meta: (clamp(i, meta), 0, 0)))
+
+    def result(self, idx, live, middle, vecs, patches, red):
         ch, d = self.ch, patches.shape[1]
-        rspec = (idx, pl.BlockSpec((1, 1, ch), lambda i, meta: (clamp(i, meta), 0, 0)))
-        return self.call(
+        c = self.c
+        (out,) = self.call(
+            partial(result_kernel, len(red)),
+            "result",
+            [self.by_row(idx), c(live), c(middle), w_(vecs), w_(patches)] + [c(a) for a in red],
+            [o_(patches.shape, BF)],
+            [pltpu.VMEM((ch, d), BF)],
+            flops=2 * ch * self.rows * d,
+            size=12 * self.rows * d,
+        )
+        return out
+
+    def scatter(self, idx, hi, lo, cot):
+        ch, d = self.ch, cot.shape[1]
+        (out,) = self.call(
             scatter_kernel,
             "scatter",
-            [rspec, self.c(res), self.c(hi), self.c(lo), w_(patches), w_(cot)],
-            [o_(patches.shape, BF), o_(patches.shape, F32)],
-            flops=6 * ch * self.rows * d,
+            [self.by_row(idx), self.c(hi), self.c(lo), w_(cot)],
+            [o_(cot.shape, F32)],
+            flops=4 * ch * self.rows * d,
             size=12 * self.rows * d,
         )
+        return out
 
 
 CODES = 169
@@ -1202,9 +1322,11 @@
         ff_own, ff_peer = ff[:2], ff[2:]
         fx, fy = first_leg(ff_own, ff_peer)
         dq1, gk1, gs1, dba1, drel1 = local.back(ag, *held[1], first, w_out[1])
-        fx, fy, dq1, gs1, ag = lax.optimization_barrier((fx, fy, dq1, gs1, ag))
+        dq1, gs1, red0 = lax.optimization_barrier((dq1, gs1, red0))
+        got1 = swap(gs1, "core", 2)
+        result = local.result(idx, live, middle, vecs, patches, [red0, red1])
+        fx, fy, dq1, result, ag = lax.optimization_barrier((fx, fy, dq1, result, ag))
         ff_up, fy, ff_b, fx = second_leg(ff_own, ff_peer, fx, fy)
-        got1 = swap(gs1, "core", 2)
         dq0, gk0, gs0, dba0, drel0 = local.back(ag, *held[0], first, w_out[0])
         got1, fx, fy, dq0, gs0 = lax.optimization_barrier((got1, fx, fy, dq0, gs0))
         at_peer = split(gk1, got1)
@@ -1213,59 +1335,73 @@
         ff_keep, ff_send = z_first(ff_up, fy, ff_b, fx)
         ff_got = swap(ff_send, "z", nz, 1)
         mg, *at4, ff_keep, ff_send = lax.optimization_barrier((mg, *at_own, *at_peer, ff_keep, ff_send))
-        res, hi, lo, v1 = local.ends(live, xc, cotc, middle, mg, vecs, [red0, red1], [dq0, dq1], w_att)
-        ax, ay, ff_got, res = lax.optimization_barrier((ax, ay, ff_got, res))
-        up, ay, own_b, ax = second_leg(at_own, at_peer, ax, ay)
+        hi, lo, v1 = local.ends(live, xc, cotc, mg, vecs, [dq0, dq1], w_att)
+        ff_got, hi = lax.optimization_barrier((ff_got, hi))
         ff_keep, ff_send = z_second(ff_keep, ff_got)
         ff_got = swap(ff_send, "z", nz, 2)
+        ax, ay, hi, ff_send = lax.optimization_barrier((ax, ay, hi, ff_send))
+        up, ay, own_b, ax = second_leg(at_own, at_peer, ax, ay)
         v1, up, own_b, ff_keep, ff_send = lax.optimization_barrier((v1, up, own_b, ff_keep, ff_send))
         mine, other = pack(t.reshape(1).astype(jnp.int32), v1, v2, (db0, db1), (dba0, dba1), (drel0, drel1))
-        ff_got, ax, ay, mine, other = lax.optimization_barrier((ff_got, ax, ay, mine, other))
         ids = jnp.stack([c, y, z]).astype(jnp.int32)
+        barrier = lambda *xs: lax.optimization_barrier(xs)
+        ax, ay, mine, other = barrier(ax, ay, mine, other)
         keep, send = z_first(up, ay, own_b, ax)
         got = swap(send, "z", nz, 1)
+        tiny_got = swap(other.astype(BF), "tensor", nt)
+        ff_got, keep, send = barrier(ff_got, keep, send)
         ff = plus(ff_keep, ff_got)
         ff2 = swap(ff, "z", nz, 2)
-        tiny = plus(mine, swap(other.astype(BF), "tensor", nt))
-        keep, ff, got, tiny = lax.optimization_barrier((keep, ff, got, tiny))
+        got, tiny_got, ff = barrier(got, tiny_got, ff)
         keep, send = z_second(keep, got)
         got = swap(send, "z", nz, 2)
-        tiny = plus(tiny, swap(tiny, "core", 2))
-        keep, send, ff2, got, tiny = lax.optimization_barrier((keep, send, ff2, got, tiny))
+        tiny = plus(mine, tiny_got)
+        tiny_got = swap(tiny, "core", 2)
+        ff2, send, tiny, tiny_got = barrier(ff2, send, tiny, tiny_got)
         ff = jnp.stack([ff, ff2])
+        ff1 = swap(ff, "z", nz, 1)
+        tiny = plus(tiny, tiny_got)
+        tiny_got = swap(tiny, "y", 2)
+        got, ff, tiny = barrier(got, ff, tiny)
         att = plus(keep, got)
-        ff1 = swap(ff, "z", nz, 1)
         att_y = swap(att, "y", 2)
-        tiny = plus(tiny, swap(tiny, "y", 2))
-        ff, att, att_y, tiny = lax.optimization_barrier((ff, att, att_y, tiny))
+        att, att_y, tiny_got = barrier(att, att_y, tiny_got)
         att = jnp.stack([att, att_y])
-        att2 = swap(att, "z", nz, 2)
-        tiny = plus(tiny, swap(tiny, "z", nz, 1))
-        att, ff1, tiny = lax.optimization_barrier((att, ff1, tiny))
+        tiny = plus(tiny, tiny_got)
+        ff1, att, tiny = barrier(ff1, att, tiny)
+        tiny_got = swap(tiny, "z", nz, 1)
         ff = jnp.concatenate([ff, ff1], 0)
         ffy = swap(ff, "y", 2)
-        tiny = plus(tiny, swap(tiny, "z", nz, 2))
-        ff, att2, tiny, res = lax.optimization_barrier((ff, att2, tiny, res))
+        att2 = swap(att, "z", nz, 2)
+        ff, att, hi, tiny = barrier(ff, att, hi, tiny)
+        input_grad = local.scatter(idx, hi, lo, cotangent)
+        tiny_got, input_grad, att = barrier(tiny_got, input_grad, att)
+        tiny = plus(tiny, tiny_got)
+        tiny_got = swap(tiny, "z", nz, 2)
+        att2, att, tiny = barrier(att2, att, tiny)
         att = jnp.stack([att, att2])
         att1 = swap(att, "z", nz, 1)
-        att, res = lax.optimization_barrier((att, res))
-        result, input_grad = local.scatter(idx, res, hi, lo, patches, cotangent)
-        att1, ffy, result = lax.optimization_barrier((att1, ffy, result))
+        tiny = plus(tiny, tiny_got).astype(F32)
+        gb_exp, gb_att = tiny[0], bias_grad(tiny[1, : 3 * GW])
+        smalls = [tiny[2 + i, : d // 2] for i in range(6)]
+        g_rel = tiny[8 : 8 + drel0.shape[0], :CODES]
+        att1, ffy, ff, att, gb_exp, gb_att, g_rel, *smalls = barrier(att1, ffy, ff, att, gb_exp, gb_att, g_rel, *smalls)
+        ff = jnp.stack([ff, ffy])
+        far = swap(ff, "core", 2)
         att = jnp.concatenate([att, att1], 0)
         att_far = swap(att, "core", 2)
-        ff, ffy, att_far = lax.optimization_barrier((ff, ffy, att_far))
-        ff = jnp.stack([ff, ffy])
-        far = swap(ff, "core", 2)
+        ff, att = barrier(ff, att)
+        g_ff = place_feed(ids, ff, d, 4 * GW)
+        far, g_ff = barrier(far, g_ff)
+        g_exp, g_red = place_feed(ids, far, d, 4 * GW, g_ff)
         g_att, g_out = place_attend(ids, att, att_far, d)
-        g_exp, g_red = place_feed(ids, ff, far, d, 4 * GW)
-        tiny = tiny.astype(F32)
-        gb_exp, gb_att = tiny[0], bias_grad(tiny[1, : 3 * GW])
-        vectors, g_rel = tiny[2:8, : d // 2], tiny[8 : 8 + drel0.shape[0], :CODES]
+        vectors = smalls
     else:
         *tiles, gb_exp, red, mg, ag, v2 = local.feed(second, branch, w_exp[0], w_red[0], b_exp[0], (live, middle, cotc, vecs, []))
         dq, ga, dba, drel = local.back(ag, *held[0], first, w_out[0])
-        res, hi, lo, v1 = local.ends(live, xc, cotc, middle, mg, vecs, [red], [dq], w_att)
-        result, input_grad = local.scatter(idx, res, hi, lo, patches, cotangent)
+        hi, lo, v1 = local.ends(live, xc, cotc, mg, vecs, [dq], w_att)
+        result = local.result(idx, live, middle, vecs, patches, [red])
+        input_grad = local.scatter(idx, hi, lo, cotangent)
         ff = jnp.concatenate(tiles, 0)
         g_exp = ff[:, 0:d].transpose(1, 0, 2).reshape(d, -1)
         g_red = ff[:, d:].transpose(0, 2, 1).reshape(-1, d)

time: 336 us -> 321 us (0.955)
  waiting for transfers between devices: 78.8 us -> 64.5 us
  local copies, waits for them, and re-layouts: 15.3 us -> 21.4 us
  Pallas kernels: 170 us -> 166 us
    ppermute x43, waiting for transfers between devices: 78.8 us -> 64.5 us  [swap(): return lax.ppermute(a, axis, [(i, i ^ step) for i in range(n)])]
    pallas_call x9 -> x10, Pallas kernels: 149 us -> 144 us  [call(): return f(self.meta, *[a for a, _ in ins])]
    unnamed x72 -> x74, local copies, waits for them, and re-layouts: 3.61 us -> 7.15 us
    pallas_call x1 -> x2, Pallas kernels: 8.77 us -> 10.3 us  [place_feed(): pl.pallas_call(place_feed_kernel, grid_spec=pltpu.PrefetchScalarGridSpec(...]
    convert_element_type x17 -> x16, other arithmetic: 16.9 us -> 16.5 us  [plus(): return total.astype(BF)]
  transfers between devices with their start and end apart: 43 -> 43, of which waited for: 20 -> 18; matrix products, arithmetic and copies ran while one was open for 10% -> 11% of each run, Pallas kernels for 49% -> 51%
where the time goes in v1:
time: 321 us; the launch traced here: 318 us
  Pallas kernels  166 us (52%)
  waiting for transfers between devices  64.5 us (20%)
  starting transfers between devices  34.2 us (11%)
  other arithmetic  29.4 us (9%)
  local copies, waits for them, and re-layouts  21.4 us (7%)
    pallas_call x10, Pallas kernels, call(): return f(self.meta, *[a for a, _ in ins])  144 us
    ppermute x43, waiting for transfers between devices, swap(): return lax.ppermute(a, axis, [(i, i ^ step) for i in range(n)])  64.5 us
    ppermute x43, starting transfers between devices, swap(): return lax.ppermute(a, axis, [(i, i ^ step) for i in range(n)])  34.2 us
    convert_element_type x16, other arithmetic, plus(): return total.astype(BF)  16.5 us
    pallas_call x2, Pallas kernels, place_feed(): pl.pallas_call(place_feed_kernel, grid_spec=pltpu.PrefetchScalarGridSpec(...  10.3 us
    unnamed x74, local copies, waits for them, and re-layouts  7.15 us
  transfers between devices with their start and end apart: 43, of which 18 were waited for; matrix products, arithmetic and copies ran while one was open for 11% of the time, Pallas kernels for 51%

profile of v1, /device:TPU:0, one launch (start us, length us, event | category | flops | bytes accessed | tf_op | source)
XLA Modules:
  0.0 317.6 jit_solution(1659364972556144294)
XLA Ops:
  0.7 3.0 collective-permute-start.3
  5.1 2.9 bound.1
  19.0 9.2 %gather_rows.1 = (bf16[1920,768]{1,0:T(8,128)(2,1)}, bf16[1920,768]{1,0:T(8,128)(2,1)}, bf16[1920,768]{1,0:T(8,128)(2,1)}, bf16[1920,768]{1,0:T(8,128)(2,1)}, f32[1920,1]{1,0:T(8,128)}, /*index=5*/s32[3,1,640]{2,1,0:T(1,128)}) custom-call(s32[80]{0:T(128)} %plan.1.meta, s32[3,128,1]{2,1,0:T(8,128)} %constant.95.clone.refs_0_, bf16[1176,768]{1,0:T(8,128)(2,1)} %refs_4_.1, ...), custom_call_target="tpu_custom_call" | custom-call | flops 2312110080 | bytes 7225344 | tf_op jit(solution)/shard_map/gather_rows/pallas_call | solution.py:983
  28.2 2.9 collective-permute-done.2.rest_6_.rest_0_
  37.1 12.7 %attend.2 = (bf16[1920,1152]{1,0:T(8,128)(2,1)}, bf16[15,3,512,128]{3,2,1,0:T(8,128)(2,1)}, bf16[1920,384]{1,0:T(8,128)(2,1)}) custom-call(s32[80]{0:T(128)} %plan.1.meta, f32[1920,1]{1,0:T(8,128)} %get-tuple-element.176.live.rest_1_.rest_8_.rest_5_.refs_1_.refs_0_, bf16[1920,768]{1,0:T(8,128)(2,1)} %get-tuple-element.185.first.rest_2_.rest_9_.rest_6_.rest_5_, ...), custom_call_target="tpu_custom_call" | custom-call | flops 90596968 | bytes 196608 | tf_op jit(solution)/shard_map/attend/pallas_call | solution.py:983
  55.2 17.0 %attend.3 = (bf16[1920,1152]{1,0:T(8,128)(2,1)}, bf16[15,3,512,128]{3,2,1,0:T(8,128)(2,1)}, bf16[1920,384]{1,0:T(8,128)(2,1)}, f32[1920,768]{1,0:T(8,128)}, bf16[1920,768]{1,0:T(8,128)(2,1)}) custom-call(s32[80]{0:T(128)} %plan.1.meta, f32[1920,1]{1,0:T(8,128)} %get-tuple-element.176.live.rest_1_.rest_8_.rest_5_.refs_1_.refs_0_, ...), custom_call_target="tpu_custom_call" | custom-call | flops 90596968 | bytes 196608 | tf_op jit(solution)/shard_map/attend/pallas_call | solution.py:983
  72.2 3.1 collective-permute-done.9.rest_2_
  79.1 20.1 %feed.2 = (bf16[2,1536,384]{2,1,0:T(8,128)(2,1)}, bf16[2,1536,384]{2,1,0:T(8,128)(2,1)}, f32[1,1536]{1,0:T(1,128)}, bf16[1920,768]{1,0:T(8,128)(2,1)}, bf16[1920,768]{1,0:T(8,128)(2,1)}) custom-call(s32[80]{0:T(128)} %plan.1.meta, bf16[1920,768]{1,0:T(8,128)(2,1)} %get-tuple-element.194.second, bf16[1920,768]{1,0:T(8,128)(2,1)} %get-tuple-element.195.branch, ...), custom_call_target="tpu_custom_call" | custom-call | flops 9059696640 | bytes 9437184 | tf_op jit(solution)/shard_map/feed/pallas_call | solution.py:983
  99.3 22.2 %feed.3 = (bf16[2,1536,384]{2,1,0:T(8,128)(2,1)}, bf16[2,1536,384]{2,1,0:T(8,128)(2,1)}, f32[1,1536]{1,0:T(1,128)}, bf16[1920,768]{1,0:T(8,128)(2,1)}, f32[1920,...) custom-call(s32[80]{0:T(128)} %plan.1.meta, bf16[1920,768]{1,0:T(8,128)(2,1)} %get-tuple-element.194.second, ...), custom_call_target="tpu_custom_call" | custom-call | flops 9059696640 | bytes 9437184 | tf_op jit(solution)/shard_map/feed/pallas_call | solution.py:983
  123.4 3.1 add_convert_fusion.2
  130.6 16.3 %back.2 = (bf16[1920,1152]{1,0:T(8,128)(2,1)}, bf16[2,768,384]{2,1,0:T(8,128)(2,1)}, bf16[2,768,384]{2,1,0:T(8,128)(2,1)}, f32[1,1152]{1,0:T(1,128)}, f32[12,256]{1,0:T(8,128)}) custom-call(s32[80]{0:T(128)} %plan.1.meta, bf16[1920,768]{1,0:T(8,128)(2,1)} %get-tuple-element.224.ag.rest_2_.rest_1_, bf16[384,384]{1,0:T(8,128)(2,1)} %constant.92.clone.perm, ...), custom_call_target="tpu_custom_call" | custom-call | flops 7927234560 | bytes 14745600 | tf_op jit(solution)/shard_map/back/pallas_call | solution.py:983
  147.0 8.2 %result.1 = bf16[1176,768]{1,0:T(8,128)(2,1)} custom-call(s32[80]{0:T(128)} %plan.1.meta, s32[3,1,640]{2,1,0:T(1,128)} %get-tuple-element.219.refs_0_, f32[1920,1]{1,0:T(8,128)} %get-tuple-element.176.live.rest_1_.rest_8_.rest_5_.refs_1_.refs_0_, f32[1920,768]{1,0:T(8,128)} %get-tuple-element.199.rest_6_.refs_2_, ...), custom_call_target="tpu_custom_call" | custom-call | flops 1156055040 | bytes 10838016 | tf_op jit(solution)/shard_map/result/pallas_call | solution.py:983
  155.2 2.6 collective-permute-done.17
  161.6 2.0 fusion.2
  164.2 17.1 %back.3 = (bf16[1920,1152]{1,0:T(8,128)(2,1)}, bf16[2,768,384]{2,1,0:T(8,128)(2,1)}, bf16[2,768,384]{2,1,0:T(8,128)(2,1)}, f32[1,1152]{1,0:T(1,128)}, f32[12,256]{1,0:T(8,128)}) custom-call(s32[80]{0:T(128)} %plan.1.meta, bf16[1920,768]{1,0:T(8,128)(2,1)} %get-tuple-element.224.ag.rest_2_.rest_1_, bf16[384,384]{1,0:T(8,128)(2,1)} %constant.92.clone.perm, ...), custom_call_target="tpu_custom_call" | custom-call | flops 7927234560 | bytes 14745600 | tf_op jit(solution)/shard_map/back/pallas_call | solution.py:983
  182.2 2.8 add_convert_fusion.6
  186.5 2.8 broadcast_select_fusion.1
  194.0 11.2 %ends.1 = (bf16[1920,768]{1,0:T(8,128)(2,1)}, bf16[1920,768]{1,0:T(8,128)(2,1)}, f32[8,768]{1,0:T(8,128)}) custom-call(s32[80]{0:T(128)} %plan.1.meta, f32[1920,1]{1,0:T(8,128)} %get-tuple-element.176.live.rest_1_.rest_8_.rest_5_.refs_1_.refs_0_, bf16[1920,768]{1,0:T(8,128)(2,1)} %get-tuple-element.188.rest_2_.rest_10_.refs_1_, ...), custom_call_target="tpu_custom_call" | custom-call | flops 2264924160 | bytes 14745600 | tf_op jit(solution)/shard_map/ends/pallas_call | solution.py:983
  211.8 2.6 collective-permute-start.29
  218.8 7.1 %collective-permute-done.29 = bf16[384,384]{1,0:T(8,128)(2,1)S(1)} collective-permute-done((bf16[384,384]{1,0:T(8,128)(2,1)}, bf16[384,384]{1,0:T(8,128)(2,1)S(1)}, u32[]{:S(2)}, u32[]{:S(2)}) %collective-permute-start.29) | collective-permute-done | bytes 294944 | tf_op jit(solution)/shard_map/ppermute | solution.py:1193
  227.6 2.8 collective-permute-done.28
  230.8 14.6 %collective-permute-done.30 = bf16[384,384]{1,0:T(8,128)(2,1)S(1)} collective-permute-done((bf16[384,384]{1,0:T(8,128)(2,1)S(1)}, bf16[384,384]{1,0:T(8,128)(2,1)S(1)}, u32[]{:S(2)}, u32[]{:S(2)}) %collective-permute-start.30) | collective-permute-done | bytes 294944 | tf_op jit(solution)/shard_map/ppermute | solution.py:1193
  245.6 3.0 collective-permute-done.33
  250.8 5.3 %collective-permute-done.35 = bf16[24,1536]{1,0:T(8,128)(2,1)S(1)} collective-permute-done((bf16[24,1536]{1,0:T(8,128)(2,1)S(1)}, bf16[24,1536]{1,0:T(8,128)(2,1)S(1)}, u32[]{:S(2)}, u32[]{:S(2)}) %collective-permute-start.35) | collective-permute-done | bytes 73760 | tf_op jit(solution)/shard_map/ppermute | solution.py:1193
  256.1 9.3 %collective-permute-done.32 = bf16[2,384,384]{2,1,0:T(8,128)(2,1)S(1)} collective-permute-done((bf16[2,384,384]{2,1,0:T(8,128)(2,1)S(1)}, bf16[2,384,384]{2,1,0:T(8,128)(2,1)S(1)}, u32[]{:S(2)}, u32[]{:S(2)}) %collective-permute-start.32) | collective-permute-done | bytes 589856 | tf_op jit(solution)/shard_map/ppermute | solution.py:1193
  265.7 2.6 collective-permute-start.37
  269.8 9.6 %scatter.1 = f32[1176,768]{1,0:T(8,128)} custom-call(s32[80]{0:T(128)} %plan.1.meta, s32[3,1,640]{2,1,0:T(1,128)} %get-tuple-element.219.refs_0_, bf16[1920,768]{1,0:T(8,128)(2,1)} %get-tuple-element.284.refs_1_, bf16[1920,768]{1,0:T(8,128)(2,1)} %get-tuple-element.285.refs_2_, bf16[1176,768]{1,0:T(8,128)(2,1)} %refs_3_.1), custom_call_target="tpu_custom_call" | custom-call | flops 2312110080 | bytes 10838016 | tf_op jit(solution)/shard_map/scatter/pallas_call | solution.py:983
  281.7 3.8 %collective-permute-done.40 = bf16[24,1536]{1,0:T(8,128)(2,1)S(1)} collective-permute-done((bf16[24,1536]{1,0:T(8,128)(2,1)S(1)}, bf16[24,1536]{1,0:T(8,128)(2,1)S(1)}, u32[]{:S(2)}, u32[]{:S(2)}) %collective-permute-start.40) | collective-permute-done | bytes 73760 | tf_op jit(solution)/shard_map/ppermute | solution.py:1193
  291.9 3.8 %collective-permute-done.38 = bf16[2,2,192,384]{3,2,1,0:T(8,128)(2,1)S(1)} collective-permute-done((bf16[2,2,192,384]{3,2,1,0:T(8,128)(2,1)S(1)}, bf16[2,2,192,384]{3,2,1,0:T(8,128)(2,1)S(1)}, u32[]{:S(2)}, u32[]{:S(2)}) %collective-permute-start.38) | collective-permute-done | bytes 589856 | tf_op jit(solution)/shard_map/ppermute | solution.py:1193
  300.9 5.2 %place_feed.2 = (f32[768,1536]{1,0:T(8,128)}, f32[1536,768]{1,0:T(8,128)}) custom-call(s32[3]{0:T(128)} %pad_add_fusion.1.ids, bf16[2,4,384,384]{3,2,1,0:T(8,128)(2,1)} %copy-done.1, bf16[2,4,384,384]{3,2,1,0:T(8,128)(2,1)} %copy-done.1), custom_call_target="tpu_custom_call" | custom-call | tf_op jit(solution)/shard_map/place_feed/pallas_call | solution.py:856
  306.1 6.1 %place_attend.1 = (f32[768,1152]{1,0:T(8,128)}, f32[384,768]{1,0:T(8,128)}) custom-call(s32[3]{0:T(128)} %pad_add_fusion.1.ids, bf16[4,2,192,384]{3,2,1,0:T(8,128)(2,1)} %copy-done, bf16[4,2,192,384]{3,2,1,0:T(8,128)(2,1)} %copy-done, bf16[4,2,192,384]{3,2,1,0:T(8,128)(2,1)} %copy-done, bf16[4,2,192,384]{3,2,1,0:T(8,128)(2,1)} %copy-done, ...), custom_call_target="tpu_custom_call" | custom-call | tf_op jit(solution)/shard_map/place_attend/pallas_call | solution.py:893
  312.2 5.2 %place_feed.3 = (f32[768,1536]{1,0:T(8,128)}, f32[1536,768]{1,0:T(8,128)}) custom-call(s32[3]{0:T(128)} %pad_add_fusion.1.ids, bf16[2,4,384,384]{3,2,1,0:T(8,128)(2,1)} %collective-permute-done.42.a.b, bf16[2,4,384,384]{3,2,1,0:T(8,128)(2,1)} %collective-permute-done.42.a.b, ...), custom_call_target="tpu_custom_call", output_to_operand_aliasing={{0}: (3, {}), {1}: (4, {})} | custom-call | tf_op jit(solution)/shard_map/place_feed/pallas_call | solution.py:856
  (209 shorter events, 76.0 us)
Async XLA Ops:
  0.7 27.5 %collective-permute-start.3 = (bf16[12,2,32]{2,1,0:T(2,128)(2,1)}, bf16[12,2,32]{2,1,0:T(2,128)(2,1)S(1)}, u32[]{:S(2)}, u32[]{:S(2)}) collective-permute-start(bf16[12,2,32]{2,1,0:T(2,128)(2,1)} %param.25), channel_id=1, source_target_pairs={{0,1},{1,0},{2,3},{3,2},{4,5},{5,4},{6,7},{7,6},{8,9},{9,8},{10,11... | collective-permute-start | bytes 4616 | tf_op jit(solution)/shard_map/ppermute | solution.py:1193
  8.0 20.2 %collective-permute-start.5 = (bf16[1536]{0:T(1024)(128)(2,1)S(1)}, bf16[1536]{0:T(1024)(128)(2,1)S(1)}, u32[]{:S(2)}, u32[]{:S(2)}) collective-permute-start(bf16[1536]{0:T(1024)(128)(2,1)S(1)} %copy-done.26), channel_id=1, source_target_pairs={{0,1},{1,0},{2,3},{3,2},{4,5},{5,4},{6,7},{7,6},{8,9},{9,8},{10,11... | collective-permute-start | bytes 9224 | tf_op jit(solution)/shard_map/ppermute | solution.py:1193
  10.1 18.1 %collective-permute-start.4 = (f32[12,256]{1,0:T(8,128)S(1)}, f32[12,256]{1,0:T(8,128)S(1)}, u32[]{:S(2)}, u32[]{:S(2)}) collective-permute-start(f32[12,256]{1,0:T(8,128)S(1)} %pad_convert_fusion.rel), channel_id=1, source_target_pairs={{0,1},{1,0},{2,3},{3,2},{4,5},{5,4},{6,7},{7,6},{8,9},{9,8},{10,11... | collective-permute-start | bytes 36872 | tf_op jit(solution)/shard_map/ppermute | solution.py:1193
  13.7 17.5 %collective-permute-start.1 = (bf16[192,1152]{1,0:T(8,128)(2,1)S(1)}, bf16[192,1152]{1,0:T(8,128)(2,1)S(1)}, u32[]{:S(2)}, u32[]{:S(2)}) collective-permute-start(bf16[192,1152]{1,0:T(8,128)(2,1)S(1)} %constant_dynamic-slice_fusion.3), channel_id=1, source_target_pairs={{0,1},{1,0},{2,3},{3,2},{4,5},{5,4},{6,7},{7,6},{8,9},{9,8},{10,11... | collective-permute-start | bytes 1327112 | tf_op jit(solution)/shard_map/ppermute | solution.py:1193
  15.7 15.4 %collective-permute-start.2 = (bf16[384,384]{1,0:T(8,128)(2,1)S(1)}, bf16[384,384]{1,0:T(8,128)(2,1)S(1)}, u32[]{:S(2)}, u32[]{:S(2)}) collective-permute-start(bf16[384,384]{1,0:T(8,128)(2,1)S(1)} %constant_dynamic-slice_fusion.2), channel_id=1, source_target_pairs={{0,1},{1,0},{2,3},{3,2},{4,5},{5,4},{6,7},{7,6},{8,9},{9,8},{10,11... | collective-permute-start | bytes 884744 | tf_op jit(solution)/shard_map/ppermute | solution.py:1193
  31.1 18.7 %collective-permute-start.7 = (bf16[768,384]{1,0:T(8,128)(2,1)S(1)}, bf16[768,384]{1,0:T(8,128)(2,1)}, u32[]{:S(2)}, u32[]{:S(2)}) collective-permute-start(bf16[768,384]{1,0:T(8,128)(2,1)S(1)} %constant_dynamic-slice_fusion.1), channel_id=1, source_target_pairs={{0,1},{1,0},{2,3},{3,2},{4,5},{5,4},{6,7},{7,6},{8,9},{9,8},{10,11... | collective-permute-start | bytes 1769480 | tf_op jit(solution)/shard_map/ppermute | solution.py:1193
  34.2 15.6 %collective-permute-start.6 = (bf16[192,1152]{1,0:T(8,128)(2,1)S(1)}, bf16[192,1152]{1,0:T(8,128)(2,1)S(1)}, u32[]{:S(2)}, u32[]{:S(2)}) collective-permute-start(bf16[192,1152]{1,0:T(8,128)(2,1)S(1)} %collective-permute-done.1), channel_id=1, source_target_pairs={{0,4},{4,0},{1,5},{5,1},{2,6},{6,2},{3,7},{7,3},{8,12},{12,8},{9,1... | collective-permute-start | bytes 1327112 | tf_op jit(solution)/shard_map/ppermute | solution.py:1193
  50.1 25.2 %collective-permute-start.9 = (bf16[768,768]{1,0:T(8,128)(2,1)S(1)}, bf16[768,768]{1,0:T(8,128)(2,1)}, u32[]{:S(2)}, u32[]{:S(2)}) collective-permute-start(bf16[768,768]{1,0:T(8,128)(2,1)S(1)} %constant_dynamic-slice_fusion), channel_id=1, source_target_pairs={{0,1},{1,0},{2,3},{3,2},{4,5},{5,4},{6,7},{7,6},{8,9},{9,8},{10,11... | collective-permute-start | bytes 3538952 | tf_op jit(solution)/shard_map/ppermute | solution.py:1193
  50.7 21.5 %collective-permute-start.8 = (bf16[768,384]{1,0:T(8,128)(2,1)}, bf16[768,384]{1,0:T(8,128)(2,1)}, u32[]{:S(2)}, u32[]{:S(2)}) collective-permute-start(bf16[768,384]{1,0:T(8,128)(2,1)} %collective-permute-done.7), channel_id=1, source_target_pairs={{0,4},{4,0},{1,5},{5,1},{2,6},{6,2},{3,7},{7,3},{8,12},{12,8},{9,1... | collective-permute-start | bytes 1769480 | tf_op jit(solution)/shard_map/ppermute | solution.py:1193
  77.3 22.0 %collective-permute-start.12 = (bf16[768,768]{1,0:T(8,128)(2,1)S(1)}, bf16[768,768]{1,0:T(8,128)(2,1)}, u32[]{:S(2)}, u32[]{:S(2)}) collective-permute-start(bf16[768,768]{1,0:T(8,128)(2,1)S(1)} %maximum_select_fusion.rest_0_), channel_id=1, source_target_pairs={{0,2},{2,0},{1,3},{3,1},{4,6},{6,4},{5,7},{7,5},{8,10},{10,8},{9,1... | collective-permute-start | bytes 3538952 | tf_op jit(solution)/shard_map/ppermute | solution.py:1193
  77.4 21.9 %collective-permute-start.13 = (bf16[768,768]{1,0:T(8,128)(2,1)}, bf16[768,768]{1,0:T(8,128)(2,1)}, u32[]{:S(2)}, u32[]{:S(2)}) collective-permute-start(bf16[768,768]{1,0:T(8,128)(2,1)} %collective-permute-done.9.rest_2_), channel_id=1, source_target_pairs={{0,2},{2,0},{1,3},{3,1},{4,6},{6,4},{5,7},{7,5},{8,10},{10,8},{9,1... | collective-permute-start | bytes 3538952 | tf_op jit(solution)/shard_map/ppermute | solution.py:1193
  99.1 22.8 %collective-permute-start.14 = (bf16[2,1536,384]{2,1,0:T(8,128)(2,1)}, bf16[2,1536,384]{2,1,0:T(8,128)(2,1)S(1)}, u32[]{:S(2)}, u32[]{:S(2)}) collective-permute-start(bf16[2,1536,384]{2,1,0:T(8,128)(2,1)} %get-tuple-element.205), channel_id=1, source_target_pairs={{0,2},{2,0},{1,3},{3,1},{4,6},{6,4},{5,7},{7,5},{8,10},{10,8},{9,1... | collective-permute-start | bytes 7077896 | tf_op jit(solution)/shard_map/ppermute | solution.py:1193
  129.4 28.5 %collective-permute-start.17 = (bf16[2,768,384]{2,1,0:T(8,128)(2,1)}, bf16[2,768,384]{2,1,0:T(8,128)(2,1)}, u32[]{:S(2)}, u32[]{:S(2)}) collective-permute-start(bf16[2,768,384]{2,1,0:T(8,128)(2,1)} %pad_maximum_fusion.1), channel_id=1, source_target_pairs={{0,4},{4,0},{1,5},{5,1},{2,6},{6,2},{3,7},{7,3},{8,12},{12,8},{9,1... | collective-permute-start | bytes 3538952 | tf_op jit(solution)/shard_map/ppermute | solution.py:1193
  130.0 28.2 %collective-permute-start.16 = (bf16[2,768,384]{2,1,0:T(8,128)(2,1)}, bf16[2,768,384]{2,1,0:T(8,128)(2,1)}, u32[]{:S(2)}, u32[]{:S(2)}) collective-permute-start(bf16[2,768,384]{2,1,0:T(8,128)(2,1)} %get-tuple-element.208), channel_id=1, source_target_pairs={{0,1},{1,0},{2,3},{3,2},{4,5},{5,4},{6,7},{7,6},{8,9},{9,8},{10,11... | collective-permute-start | bytes 3538952 | tf_op jit(solution)/shard_map/ppermute | solution.py:1193
  146.9 34.4 %collective-permute-start.18 = (bf16[2,768,384]{2,1,0:T(8,128)(2,1)}, bf16[2,768,384]{2,1,0:T(8,128)(2,1)}, u32[]{:S(2)}, u32[]{:S(2)}) collective-permute-start(bf16[2,768,384]{2,1,0:T(8,128)(2,1)} %get-tuple-element.228), channel_id=1, source_target_pairs={{0,2},{2,0},{1,3},{3,1},{4,6},{6,4},{5,7},{7,5},{8,10},{10,8},{9,1... | collective-permute-start | bytes 3538952 | tf_op jit(solution)/shard_map/ppermute | solution.py:1193
  160.2 21.1 %collective-permute-start.20 = (bf16[768,384]{1,0:T(8,128)(2,1)}, bf16[768,384]{1,0:T(8,128)(2,1)}, u32[]{:S(2)}, u32[]{:S(2)}) collective-permute-start(bf16[768,384]{1,0:T(8,128)(2,1)} %fusion.3), channel_id=1, source_target_pairs={{0,4},{4,0},{1,5},{5,1},{2,6},{6,2},{3,7},{7,3},{8,12},{12,8},{9,1... | collective-permute-start | bytes 1769480 | tf_op jit(solution)/shard_map/ppermute | solution.py:1193
  163.6 17.7 %collective-permute-start.19 = (bf16[768,384]{1,0:T(8,128)(2,1)}, bf16[768,384]{1,0:T(8,128)(2,1)S(1)}, u32[]{:S(2)}, u32[]{:S(2)}) collective-permute-start(bf16[768,384]{1,0:T(8,128)(2,1)} %fusion.2), channel_id=1, source_target_pairs={{0,1},{1,0},{2,3},{3,2},{4,5},{5,4},{6,7},{7,6},{8,9},{9,8},{10,11... | collective-permute-start | bytes 1769480 | tf_op jit(solution)/shard_map/ppermute | solution.py:1193
  181.3 9.5 %collective-permute-start.21 = (bf16[2,768,384]{2,1,0:T(8,128)(2,1)}, bf16[2,768,384]{2,1,0:T(8,128)(2,1)}, u32[]{:S(2)}, u32[]{:S(2)}) collective-permute-start(bf16[2,768,384]{2,1,0:T(8,128)(2,1)} %get-tuple-element.234), channel_id=1, source_target_pairs={{0,2},{2,0},{1,3},{3,1},{4,6},{6,4},{5,7},{7,5},{8,10},{10,8},{9,1... | collective-permute-start | bytes 3538952 | tf_op jit(solution)/shard_map/ppermute | solution.py:1193
  185.0 21.1 %collective-permute-start.22 = (bf16[2,384,384]{2,1,0:T(8,128)(2,1)}, bf16[2,384,384]{2,1,0:T(8,128)(2,1)}, u32[]{:S(2)}, u32[]{:S(2)}) collective-permute-start(bf16[2,384,384]{2,1,0:T(8,128)(2,1)} %get-tuple-element.332), channel_id=1, source_target_pairs={{0,1},{1,0},{2,3},{3,2},{4,5},{5,4},{6,7},{7,6},{8,9},{9,8},{10,11... | collective-permute-start | bytes 1769480 | tf_op jit(solution)/shard_map/ppermute | solution.py:1193
  189.3 16.0 %collective-permute-start.24 = (bf16[768,384]{1,0:T(8,128)(2,1)}, bf16[768,384]{1,0:T(8,128)(2,1)S(1)}, u32[]{:S(2)}, u32[]{:S(2)}) collective-permute-start(bf16[768,384]{1,0:T(8,128)(2,1)} %get-tuple-element.326), channel_id=1, source_target_pairs={{0,8},{8,0},{16,24},{24,16},{1,9},{9,1},{17,25},{25,17},{2,10},{10... | collective-permute-start | bytes 1769480 | tf_op jit(solution)/shard_map/ppermute | solution.py:1193
  193.3 14.8 %collective-permute-start.23 = (bf16[2,384,384]{2,1,0:T(8,128)(2,1)}, bf16[2,384,384]{2,1,0:T(8,128)(2,1)}, u32[]{:S(2)}, u32[]{:S(2)}) collective-permute-start(bf16[2,384,384]{2,1,0:T(8,128)(2,1)} %pad_maximum_fusion.2), channel_id=1, source_target_pairs={{0,4},{4,0},{1,5},{5,1},{2,6},{6,2},{3,7},{7,3},{8,12},{12,8},{9,1... | collective-permute-start | bytes 1769480 | tf_op jit(solution)/shard_map/ppermute | solution.py:1193
  211.8 14.1 %collective-permute-start.29 = (bf16[384,384]{1,0:T(8,128)(2,1)}, bf16[384,384]{1,0:T(8,128)(2,1)S(1)}, u32[]{:S(2)}, u32[]{:S(2)}) collective-permute-start(bf16[384,384]{1,0:T(8,128)(2,1)} %get-tuple-element.338), channel_id=1, source_target_pairs={{0,16},{8,24},{16,0},{24,8},{1,17},{9,25},{17,1},{25,9},{2,18},{10... | collective-permute-start | bytes 884744 | tf_op jit(solution)/shard_map/ppermute | solution.py:1193
  218.3 12.3 %collective-permute-start.27 = (bf16[384,384]{1,0:T(8,128)(2,1)S(1)}, bf16[384,384]{1,0:T(8,128)(2,1)S(1)}, u32[]{:S(2)}, u32[]{:S(2)}) collective-permute-start(bf16[384,384]{1,0:T(8,128)(2,1)S(1)} %get-tuple-element.335), channel_id=1, source_target_pairs={{0,8},{8,0},{16,24},{24,16},{1,9},{9,1},{17,25},{25,17},{2,10},{10... | collective-permute-start | bytes 884744 | tf_op jit(solution)/shard_map/ppermute | solution.py:1193
  227.5 18.0 %collective-permute-start.30 = (bf16[384,384]{1,0:T(8,128)(2,1)S(1)}, bf16[384,384]{1,0:T(8,128)(2,1)S(1)}, u32[]{:S(2)}, u32[]{:S(2)}) collective-permute-start(bf16[384,384]{1,0:T(8,128)(2,1)S(1)} %add_convert_fusion.12), channel_id=1, source_target_pairs={{0,16},{8,24},{16,0},{24,8},{1,17},{9,25},{17,1},{25,9},{2,18},{10... | collective-permute-start | bytes 884744 | tf_op jit(solution)/shard_map/ppermute | solution.py:1193
  230.6 14.9 %collective-permute-start.31 = (bf16[24,1536]{1,0:T(8,128)(2,1)S(1)}, bf16[24,1536]{1,0:T(8,128)(2,1)S(1)}, u32[]{:S(2)}, u32[]{:S(2)}) collective-permute-start(bf16[24,1536]{1,0:T(8,128)(2,1)S(1)} %add_convert_fusion.28), channel_id=1, source_target_pairs={{0,2},{2,0},{1,3},{3,1},{4,6},{6,4},{5,7},{7,5},{8,10},{10,8},{9,1... | collective-permute-start | bytes 221192 | tf_op jit(solution)/shard_map/ppermute | solution.py:1193
  230.8 17.8 %collective-permute-start.33 = (bf16[192,384]{1,0:T(8,128)(2,1)S(1)}, bf16[192,384]{1,0:T(8,128)(2,1)S(1)}, u32[]{:S(2)}, u32[]{:S(2)}) collective-permute-start(bf16[192,384]{1,0:T(8,128)(2,1)S(1)} %add_convert_fusion.23), channel_id=1, source_target_pairs={{0,16},{8,24},{16,0},{24,8},{1,17},{9,25},{17,1},{25,9},{2,18},{10... | collective-permute-start | bytes 442376 | tf_op jit(solution)/shard_map/ppermute | solution.py:1193
  250.7 14.7 %collective-permute-start.32 = (bf16[2,384,384]{2,1,0:T(8,128)(2,1)S(1)}, bf16[2,384,384]{2,1,0:T(8,128)(2,1)S(1)}, u32[]{:S(2)}, u32[]{:S(2)}) collective-permute-start(bf16[2,384,384]{2,1,0:T(8,128)(2,1)S(1)} %pad_maximum_fusion.3), channel_id=1, source_target_pairs={{0,8},{8,0},{16,24},{24,16},{1,9},{9,1},{17,25},{25,17},{2,10},{10... | collective-permute-start | bytes 1769480 | tf_op jit(solution)/shard_map/ppermute | solution.py:1193
  265.4 14.0 %collective-permute-start.36 = (bf16[24,1536]{1,0:T(8,128)(2,1)S(1)}, bf16[24,1536]{1,0:T(8,128)(2,1)S(1)}, u32[]{:S(2)}, u32[]{:S(2)}) collective-permute-start(bf16[24,1536]{1,0:T(8,128)(2,1)S(1)} %add_convert_fusion.26), channel_id=1, source_target_pairs={{0,8},{8,0},{16,24},{24,16},{1,9},{9,1},{17,25},{25,17},{2,10},{10... | collective-permute-start | bytes 221192 | tf_op jit(solution)/shard_map/ppermute | solution.py:1193
  265.7 14.7 %collective-permute-start.37 = (bf16[2,192,384]{2,1,0:T(8,128)(2,1)S(1)}, bf16[2,192,384]{2,1,0:T(8,128)(2,1)S(1)}, u32[]{:S(2)}, u32[]{:S(2)}) collective-permute-start(bf16[2,192,384]{2,1,0:T(8,128)(2,1)S(1)} %pad_maximum_fusion.5), channel_id=1, source_target_pairs={{0,16},{8,24},{16,0},{24,8},{1,17},{9,25},{17,1},{25,9},{2,18},{10... | collective-permute-start | bytes 884744 | tf_op jit(solution)/shard_map/ppermute | solution.py:1193
  268.4 27.3 %collective-permute-start.39 = (bf16[4,384,384]{2,1,0:T(8,128)(2,1)S(1)}, bf16[4,384,384]{2,1,0:T(8,128)(2,1)S(1)}, u32[]{:S(2)}, u32[]{:S(2)}) collective-permute-start(bf16[4,384,384]{2,1,0:T(8,128)(2,1)S(1)} %constant_dynamic-update-slice_fusion), channel_id=1, source_target_pairs={{0,4},{4,0},{1,5},{5,1},{2,6},{6,2},{3,7},{7,3},{8,12},{12,8},{9,1... | collective-permute-start | bytes 3538952 | tf_op jit(solution)/shard_map/ppermute | solution.py:1193
  280.5 15.2 %collective-permute-start.38 = (bf16[2,2,192,384]{3,2,1,0:T(8,128)(2,1)S(1)}, bf16[2,2,192,384]{3,2,1,0:T(8,128)(2,1)S(1)}, u32[]{:S(2)}, u32[]{:S(2)}) collective-permute-start(bf16[2,2,192,384]{3,2,1,0:T(8,128)(2,1)S(1)} %pad_maximum_fusion.4), channel_id=1, source_target_pairs={{0,8},{8,0},{16,24},{24,16},{1,9},{9,1},{17,25},{25,17},{2,10},{10... | collective-permute-start | bytes 1769480 | tf_op jit(solution)/shard_map/ppermute | solution.py:1193
  298.5 13.7 %collective-permute-start.42 = (bf16[2,4,384,384]{3,2,1,0:T(8,128)(2,1)S(1)}, bf16[2,4,384,384]{3,2,1,0:T(8,128)(2,1)}, u32[]{:S(2)}, u32[]{:S(2)}) collective-permute-start(bf16[2,4,384,384]{3,2,1,0:T(8,128)(2,1)S(1)} %pad_maximum_fusion.a.b), channel_id=1, source_target_pairs={{0,2},{2,0},{1,3},{3,1},{4,6},{6,4},{5,7},{7,5},{8,10},{10,8},{9,1... | collective-permute-start | bytes 7077896 | tf_op jit(solution)/shard_map/ppermute | solution.py:1193
  (47 other events, 268.1 us)
